TPU v7x, 256 devices: a whole 4x4x8 slice. The times are simulated.
256 devices in a mesh: gx: 8 (over x_lo, y), gy: 32 (over x_hi, z, core).
Axes of the slice: x: 4 (x_hi: 2, x_lo: 2; x = x_hi * 2 + x_lo), y: 4, z: 8, core: 2. Of those that a mesh axis runs over, the one named last changes fastest.
Arguments:
- u_face: float32 [8, 2048, 2048], P(None, 'gy', 'gx'), may hold values from -6 to 6
- v_face: float32 [8, 2048, 2048], P(None, 'gy', 'gx'), may hold values from -6 to 6
- w_face: float32 [8, 2048, 2048], P(None, 'gy', 'gx'), may hold values from -6 to 6
- theta_field: float32 [8, 2048, 2048], P(None, 'gy', 'gx'), may hold values from -6 to 6
- density: float32 [8], replicated, may hold values from 0.3 to 1.5
- thickness: float32 [8], replicated, may hold values from 4 to 32
Outputs:
- u_new: float32 [8, 2048, 2048], P(None, 'gy', 'gx')
- v_new: float32 [8, 2048, 2048], P(None, 'gy', 'gx')
- w_new: float32 [8, 2048, 2048], P(None, 'gy', 'gx')
- theta_new: float32 [8, 2048, 2048], P(None, 'gy', 'gx')
- pressure: float32 [8, 2048, 2048], P(None, 'gy', 'gx')
All inputs are finite; a program needn't handle non-finite values.
Results may differ from a plain program's by a relative error of at most 0.0003.
Values sent between devices are 32-bit elements; how exact they have to be, the bound alone decides.
A program may use at most 64 MiB of HBM per device.

v0:
```python
import functools

import jax
import jax.numpy as jnp
import numpy as np
from jax import lax
from jax.experimental import pallas as pl
from jax.experimental.pallas import tpu as pltpu
from jax.sharding import PartitionSpec as P

DT = 0.2
f32 = jnp.float32
bf16 = jnp.bfloat16
MESH = pl.DeviceIdType.MESH
C1, C2, C3 = float(np.cos(np.pi / 8)), float(np.cos(np.pi / 4)), float(np.cos(3 * np.pi / 8))
YC = 16


def split_bf16(a):
    hi = a.astype(jnp.bfloat16)
    lo = (a - hi.astype(np.float64)).astype(jnp.bfloat16)
    return hi, lo


@functools.cache
def tables():
    n_x = 2048
    l = np.arange(128)
    n = np.arange(128)

    def cas(t):
        return np.cos(t) + np.sin(t)

    cos = np.cos(2 * np.pi * np.outer(l, n) / 128)
    sin = np.sin(2 * np.pi * np.outer(l, n) / 128)
    zero = np.zeros((128, 128))
    fw = np.block([[cos, -sin], [sin, cos]])
    b0 = cas(2 * np.pi * np.outer(l, n) / 128)
    b8 = cas(2 * np.pi * np.outer(l, 16 * n + 8) / n_x)
    fb = np.block([[b0, zero], [zero, b8]])
    mats = []
    for m in (fw, fb, fw.T * (2 / n_x), fb.T * (1 / n_x)):
        mats.extend(split_bf16(m))
    mats = np.stack(mats)
    tw = np.arange(8)[:, None] * l[None, :] * (2 * np.pi / n_x)
    k_lo = 16 * n[None, :] + np.arange(8)[:, None]
    k_hi = k_lo.copy()
    k_hi[0] += 8
    tab = np.concatenate(
        [np.cos(tw), np.sin(tw), 4 * np.sin(np.pi * k_lo / n_x) ** 2, 4 * np.sin(np.pi * k_hi / n_x) ** 2]
    ).astype(np.float32)
    return mats, tab


def fwd16(x):
    s = [x[q] + x[q + 8] for q in range(8)]
    d = [x[q] - x[q + 8] for q in range(8)]
    t = [s[q] + s[q + 4] for q in range(4)]
    e = [s[q] - s[q + 4] for q in range(4)]
    t02, t13 = t[0] + t[2], t[1] + t[3]
    re, im = {}, {}
    y0, y8 = t02 + t13, t02 - t13
    re[4], im[4] = t[0] - t[2], t[3] - t[1]
    a, b = C2 * (e[1] - e[3]), C2 * (e[1] + e[3])
    re[2], re[6] = e[0] + a, e[0] - a
    im[2], im[6] = -(e[2] + b), e[2] - b
    u = [None] + [d[q] - d[8 - q] for q in (1, 2, 3)]
    v = [None] + [d[q] + d[8 - q] for q in (1, 2, 3)]
    g = C2 * u[2]
    g1, g2 = d[0] + g, d[0] - g
    h1, h2 = C1 * u[1] + C3 * u[3], C3 * u[1] - C1 * u[3]
    re[1], re[7], re[3], re[5] = g1 + h1, g1 - h1, g2 + h2, g2 - h2
    k = C2 * v[2]
    k1, k2 = k + d[4], k - d[4]
    m1, m2 = C3 * v[1] + C1 * v[3], C1 * v[1] - C3 * v[3]
    im[1], im[7], im[3], im[5] = -(m1 + k1), k1 - m1, -(m2 + k2), k2 - m2
    return y0, y8, re, im


def inv16(a0, a8, zr, zi):
    p1, m1, p3, m3 = zr[1] + zr[7], zr[1] - zr[7], zr[3] + zr[5], zr[3] - zr[5]
    r1, s1, r3, s3 = zi[1] + zi[7], zi[1] - zi[7], zi[3] + zi[5], zi[3] - zi[5]
    o = [None] * 8
    o[0] = p1 + p3
    o[4] = s3 - s1
    cs = [None, C1 * m1 + C3 * m3, C2 * (p1 - p3), C3 * m1 - C1 * m3]
    sn = [None, C3 * r1 + C1 * r3, C2 * (s1 + s3), C1 * r1 - C3 * r3]
    for q in (1, 2, 3):
        o[q] = cs[q] - sn[q]
        o[8 - q] = -cs[q] - sn[q]
    ap, am = a0 + a8, a0 - a8
    g = [ap + zr[4], am - zi[4], ap - zr[4], am + zi[4]]
    w1, w2 = C2 * (zr[2] - zr[6]), C2 * (zi[2] + zi[6])
    h = [zr[2] + zr[6], w1 - w2, zi[6] - zi[2], -w1 - w2]
    ev = [g[q] + h[q] for q in range(4)] + [g[q] - h[q] for q in range(4)]
    return [ev[q] + o[q] for q in range(8)] + [ev[q] - o[q] for q in range(8)]


def dot3(x, hi, lo):
    xh = x.astype(bf16)
    xl = (x - xh.astype(f32)).astype(bf16)
    out = jnp.dot(xh, hi, preferred_element_type=f32)
    out += jnp.dot(xl, hi, preferred_element_type=f32)
    out += jnp.dot(xh, lo, preferred_element_type=f32)
    return out


def flux(qm2, qm1, q0, q1, q2, q3, c):
    s = 37.0 * (q0 + q1) - 8.0 * (qm1 + q2) + (qm2 + q3)
    d = 10.0 * (q1 - q0) - 5.0 * (q2 - qm1) + (q3 - qm2)
    return c * s - jnp.abs(c) * d


def roll(x, shift, axis):
    n = x.shape[axis]
    shift = shift % n
    return x if shift == 0 else pltpu.roll(x, shift, axis)


def lanes(shape):
    return lax.broadcasted_iota(jnp.int32, shape, len(shape) - 1)


def rows_of(shape):
    return lax.broadcasted_iota(jnp.int32, shape, 0)


def kernel(
    nx_dev, ny_dev,
    den_ref, thk_ref, tab_ref, u_hbm, v_hbm, w_hbm, th_hbm, mats_hbm,
    un_ref, vn_ref, wn_ref, tn_ref, p_ref,
    U, V, W, TH, MATS, COEF, TF, TI, LAM,
    PE_S, PW_S, PE_R, PW_R, YN_S, YS_S, YN_R, YS_R, FPK, FYP,
    WS, SRC, TX1, RX1, Z, S, SB, IFS, IFR, IFO, IFB, RP, TX2, RX2, X2, XR, EW, EC, EX,
    in_sem, hs_sem, hr_sem, s1_sem, r1_sem, l1_sem, is_sem, ir_sem, s2_sem, r2_sem, l2_sem,
    sx_sem, rx_sem,
):
    gx = lax.axis_index("gx")
    gy = lax.axis_index("gy")
    levels, ny, nx = u_hbm.shape
    chunks = ny // YC

    def px(t):
        return lax.rem(gx + t, nx_dev)

    def py(t):
        return lax.rem(gy + t, ny_dev)

    mid = pl.ds(8, ny)
    loads = [
        pltpu.make_async_copy(w_hbm, W.at[:, mid, :], in_sem.at[0]),
        pltpu.make_async_copy(th_hbm, TH.at[:, mid, :], in_sem.at[1]),
        pltpu.make_async_copy(u_hbm, U, in_sem.at[2]),
        pltpu.make_async_copy(v_hbm, V.at[:, mid, :], in_sem.at[3]),
        pltpu.make_async_copy(mats_hbm, MATS, in_sem.at[4]),
    ]
    for cp in loads:
        cp.start()

    barrier = pltpu.get_barrier_semaphore()
    for t in range(1, nx_dev):
        pl.semaphore_signal(barrier, inc=1, device_id={"gx": px(t)}, device_id_type=MESH)

    @pl.loop(1, ny_dev)
    def _(t):
        pl.semaphore_signal(barrier, inc=1, device_id={"gy": py(t)}, device_id_type=MESH)

    r8 = rows_of((8, 128))
    j8 = lax.rem(lanes((8, 128)), 8)
    den = jnp.zeros((8, 128), f32)
    thk = jnp.zeros((8, 128), f32)
    for k in range(levels):
        den = jnp.where(r8 == k, den_ref[k], den)
        thk = jnp.where(r8 == k, thk_ref[k], thk)

    def lift(a):
        return jnp.where(r8 == 7, a, roll(a, -1, 0))

    def below(a):
        return jnp.where(r8 == 0, 0.0, roll(a, 1, 0))

    lden = lift(den)
    fd = (den + lden) / 2.0
    fs = (thk + lift(thk)) / 2.0
    mass = den * thk
    zw = (DT / 60.0) / (fd * fs)
    zt = (DT / 60.0) / mass
    sc = (1.0 / DT) / mass
    coefs = [lden * zw, below(lden) * zw, fd * zt, below(fd) * zt, fd * sc, below(fd) * sc, DT / fs]
    for i, a in enumerate(coefs):
        COEF[i * 8 : i * 8 + 8, :] = jnp.concatenate([a, a], axis=1)

    cond = fd / fs
    diag = jnp.sqrt(cond / mass)
    off = -jnp.sqrt(cond / lift(mass))
    b_mat = jnp.where(j8 == r8, diag, jnp.where(j8 == r8 + 1, off, 0.0))
    q_mat = jnp.where(j8 == r8, 1.0, 0.0)
    offsets = {}
    for r in range(1, 8):
        offsets[r] = sorted({((l ^ r) - l) % 8 for l in range(8)})

    def partner(x, r):
        out = None
        lane = j8
        for o in offsets[r]:
            moved = roll(x, -o, 1)
            sel = lax.rem(lane + o, 8) == (lane ^ r)
            out = moved if out is None else jnp.where(sel, moved, out)
        return out

    def sweep(_, carry):
        b, q = carry
        for r in range(1, 8):
            bp, qp = partner(b, r), partner(q, r)
            al = jnp.sum(b * b, axis=0, keepdims=True)
            ap = jnp.sum(bp * bp, axis=0, keepdims=True)
            g = jnp.sum(b * bp, axis=0, keepdims=True)
            d = ap - al
            lane = j8[:1]
            sg = jnp.where(d > 0.0, 2.0, jnp.where(d < 0.0, -2.0, jnp.where(lane < (lane ^ r), 2.0, -2.0)))
            t = sg * g / (jnp.abs(d) + jnp.sqrt(d * d + 4.0 * g * g) + 1e-18)
            c = 1.0 / jnp.sqrt(1.0 + t * t)
            s = c * t
            b, q = c * b - s * bp, c * q - s * qp
        return b, q

    b_mat, q_mat = lax.fori_loop(0, 5, sweep, (b_mat, q_mat))
    lam = jnp.broadcast_to(jnp.sum(b_mat * b_mat, axis=0, keepdims=True), (8, 128))
    root = jnp.sqrt(mass)
    qf = q_mat * root
    qi = q_mat / root
    for j in range(8):
        TF[j * 8 : j * 8 + 8, :] = jnp.broadcast_to(qf[:, j : j + 1], (8, 128))
        TI[j * 8 : j * 8 + 8, :] = jnp.broadcast_to(qi[:, j : j + 1], (8, 128))
        LAM[j] = jnp.broadcast_to(lam[:, j : j + 1], (8, 128))

    for cp in loads[:4]:
        cp.wait()
    lane_c = lanes((YC, 128))

    @pl.loop(0, chunks)
    def _(c):
        y0 = pl.multiple_of(c * YC, YC)
        east = jnp.zeros((YC, 128), f32)
        west = jnp.zeros((YC, 128), f32)
        for k in range(levels):
            o = 16 * k
            rows = pl.ds(y0 + 8, YC)
            wl, wr = W[k, rows, 0:128], W[k, rows, 128:256]
            tl, tr = TH[k, rows, 0:128], TH[k, rows, 128:256]
            ur = U[k, pl.ds(y0, YC), 128:256]
            east = jnp.where((lane_c >= o) & (lane_c < o + 3), roll(wr, o - 125, 1), east)
            east = jnp.where((lane_c >= o + 3) & (lane_c < o + 6), roll(tr, o + 3 - 125, 1), east)
            east = jnp.where(lane_c == o + 6, roll(ur, o + 6 - 127, 1), east)
            west = jnp.where((lane_c >= o) & (lane_c < o + 3), roll(wl, o, 1), west)
            west = jnp.where((lane_c >= o + 3) & (lane_c < o + 6), roll(tl, o + 3, 1), west)
        PE_S[pl.ds(y0, YC), :] = east
        PW_S[pl.ds(y0, YC), :] = west

    for k in range(levels):
        a, b, c = W[k, ny : ny + 8, :], TH[k, ny : ny + 8, :], V[k, ny : ny + 8, :]
        row = rows_of((8, nx))
        YN_S[k] = jnp.where(row < 3, roll(a, 3, 0), jnp.where(row < 6, roll(b, 6, 0), roll(c, 7, 0)))
        a, b = W[k, 8:16, :], TH[k, 8:16, :]
        YS_S[k] = jnp.where(row < 3, a, roll(b, 3, 0))

    pl.semaphore_wait(barrier, nx_dev + ny_dev - 2)
    halos = []
    for i, (src, dst, where) in enumerate(
        [
            (PE_S, PE_R, {"gx": px(1)}),
            (PW_S, PW_R, {"gx": px(nx_dev - 1)}),
            (YN_S, YN_R, {"gy": py(1)}),
            (YS_S, YS_R, {"gy": py(ny_dev - 1)}),
        ]
    ):
        cp = pltpu.make_async_remote_copy(
            src_ref=src, dst_ref=dst, send_sem=hs_sem.at[i], recv_sem=hr_sem.at[i],
            device_id=where, device_id_type=MESH,
        )
        cp.start()
        halos.append(cp)
    for cp in halos:
        cp.wait()

    for k in range(levels):
        n8, s8 = YN_R[k], YS_R[k]
        W[k, 0:8, :] = roll(n8, 5, 0)
        TH[k, 0:8, :] = roll(n8, 2, 0)
        V[k, 0:8, :] = roll(n8, 1, 0)
        W[k, ny + 8 : ny + 16, :] = s8
        TH[k, ny + 8 : ny + 16, :] = roll(s8, 5, 0)

    lane_n = lanes((ny, 128))
    ph, po = PE_R[...], PW_S[...]
    lane_m = lax.rem(lane_n, 16)
    u_th = roll(ph, -3, 1)
    u_top = jnp.where(lane_n >= 112, roll(ph, -6, 1), roll(ph, -22, 1))
    u_w = (roll(ph, -6, 1) + u_top) / 2.0
    FPK[...] = flux(
        ph, roll(ph, -1, 1), roll(ph, -2, 1), po, roll(po, -1, 1), roll(po, -2, 1),
        jnp.where(lane_m == 0, u_w, u_th),
    )

    def nxt(k):
        return min(k + 1, levels - 1)

    def y_shifts(block, n):
        return [roll(block, -s, 0)[8 : 8 + n] if s else block[8 : 8 + n] for s in range(-2, 4)]

    def south_flux(field, first, lifted):
        for k in range(levels):
            block = field[k, 0:16, :]
            qs = [roll(block, -s, 0)[0:8] for s in range(-2, 4)]
            c = V[k, 0:8, :]
            if lifted:
                c = (c + V[nxt(k), 0:8, :]) / 2.0
            FYP[k] = flux(*qs, c)

    def advect(field, k, y0, extra, lifted, fz_below, zi):
        o = 16 * k + extra
        rows = pl.ds(y0 + 8, YC)
        cen = pl.ds(y0, YC)
        block = field[k, pl.ds(y0, YC + 16), :]
        q = block[8 : 8 + YC]
        left, right = q[:, :128], q[:, 128:]
        pe, pw = PW_R[cen, :], PE_R[cen, :]
        ls, rs = [], []
        for s in range(-2, 4):
            if s == 0:
                ls.append(left)
                rs.append(right)
                continue
            a, b = roll(left, -s, 1), roll(right, -s, 1)
            if s > 0:
                ls.append(jnp.where(lane_c < 128 - s, a, b))
                rs.append(jnp.where(lane_c < 128 - s, b, roll(pe, -s - o, 1)))
            else:
                ls.append(jnp.where(lane_c >= -s, a, roll(pw, -s - 3 - o, 1)))
                rs.append(jnp.where(lane_c >= -s, b, a))
        u, v, w = U[k, cen, :], V[k, rows, :], W[k, rows, :]
        if lifted:
            u = (u + U[nxt(k), cen, :]) / 2.0
            v = (v + V[nxt(k), rows, :]) / 2.0
            w = (w + W[nxt(k), rows, :]) / 2.0
        fl = flux(*ls, u[:, :128])
        fr = flux(*rs, u[:, 128:])
        fl_roll = roll(fl, 1, 1)
        wl = jnp.where(lane_c >= 1, fl_roll, roll(FPK[cen, :], -o, 1))
        wr = jnp.where(lane_c >= 1, roll(fr, 1, 1), fl_roll)
        div = jnp.concatenate([fl - wl, fr - wr], axis=1)
        fy = flux(*y_shifts(block, YC), v)
        prev = roll(jnp.concatenate([FYP[k], fy], axis=0), 1, 0)[8:]
        FYP[k] = fy[YC - 8 :]
        div = div + (fy - prev)
        zq = [field[min(max(k + s, 0), levels - 1), rows, :] for s in range(-2, 4)]
        fz = flux(*zq, w)
        tend = (-DT / 60.0) * div - COEF[zi + k : zi + k + 1, :] * fz
        if k > 0:
            tend = tend + COEF[zi + 8 + k : zi + 9 + k, :] * fz_below
        return q, tend, fz

    def send(src, dst, s_sem, r_sem, who):
        return pltpu.make_async_remote_copy(
            src_ref=src, dst_ref=dst, send_sem=s_sem, recv_sem=r_sem,
            device_id=who, device_id_type=MESH,
        )

    south_flux(W, 0, True)

    @pl.loop(0, chunks)
    def _(c):
        y0 = pl.multiple_of(c * YC, YC)
        rows = pl.ds(y0 + 8, YC)
        cen = pl.ds(y0, YC)
        fz, star_below = None, None
        for k in range(levels):
            q, tend, fz = advect(W, k, y0, 0, True, fz, 0)
            star = q + tend + (0.5 * DT) * (TH[k, rows, :] + TH[nxt(k), rows, :])
            WS[k, cen, :] = star
            u = U[k, cen, :]
            ul = roll(u[:, :128], 1, 1)
            uw = jnp.where(lane_c >= 1, ul, roll(PE_R[cen, :], -(16 * k + 6), 1))
            ue = jnp.where(lane_c >= 1, roll(u[:, 128:], 1, 1), ul)
            vb = V[k, pl.ds(y0, YC + 8), :]
            dv = (vb - roll(vb, 1, 0))[8:]
            src = (u - jnp.concatenate([uw, ue], axis=1) + dv) * (1.0 / DT)
            src = src + COEF[32 + k : 33 + k, :] * star
            if k > 0:
                src = src - COEF[40 + k : 41 + k, :] * star_below
            star_below = star
            SRC[k] = src
        for h in range(2):
            hs = slice(128 * h, 128 * h + 128)
            col = [SRC[k, :, hs] for k in range(levels)]
            for j in range(levels):
                acc = TF[j * 8 : j * 8 + 1, :] * col[0]
                for k in range(1, levels):
                    acc = acc + TF[j * 8 + k : j * 8 + k + 1, :] * col[k]
                TX1[j, c, h] = acc
        pltpu.make_async_copy(TX1.at[gx, c], RX1.at[c, gx], l1_sem.at[c]).start()
        for t in range(1, nx_dev):
            g = px(t)
            send(TX1.at[g, c], RX1.at[c, gx], s1_sem.at[c, t], r1_sem.at[c, gx], {"gx": g}).start()

    south_flux(TH, 0, False)

    @pl.loop(0, chunks)
    def _(c):
        y0 = pl.multiple_of(c * YC, YC)
        fz = None
        for k in range(levels):
            q, tend, fz = advect(TH, k, y0, 3, False, fz, 16)
            tn_ref[k, pl.ds(y0, YC), :] = q + tend

    lam_g = LAM[gx]
    rate, scale = [], []
    for h in range(2):
        mu = lam_g + tab_ref[16 + 8 * h : 24 + 8 * h, :]
        rt = jnp.sqrt(mu * mu + 4.0 * mu)
        rate.append(2.0 / (2.0 + mu + rt))
        scale.append(-1.0 / rt)

    loads[4].wait()

    def x_forward(c, carry):
        y0 = pl.multiple_of(c * YC, YC)
        pltpu.make_async_copy(TX1.at[gx, c], RX1.at[c, gx], l1_sem.at[c]).wait()
        for t in range(1, nx_dev):
            g = px(t)
            send(TX1.at[g, c], RX1.at[c, g], s1_sem.at[c, t], r1_sem.at[c, g], {"gx": g}).wait_recv()
        for i in range(YC // 8):
            sub = slice(8 * i, 8 * i + 8)
            x = [RX1[c, q // 2, q % 2, sub, :] for q in range(16)]
            y_0, y_8, re, im = fwd16(x)
            Z[8 * i : 8 * i + 8, 0:128] = y_0
            Z[8 * i : 8 * i + 8, 128:256] = y_8
            for m in range(1, 8):
                co, si = tab_ref[m : m + 1, :], tab_ref[8 + m : 9 + m, :]
                at = m * YC + 8 * i
                Z[at : at + 8, 0:128] = re[m] * co + im[m] * si
                Z[at : at + 8, 128:256] = im[m] * co - re[m] * si
        o0 = dot3(Z[0:YC, :], MATS[2], MATS[3])
        om = dot3(Z[YC : 8 * YC, :], MATS[0], MATS[1])
        for m in range(8):
            val = o0 if m == 0 else om[(m - 1) * YC : m * YC]
            for h in range(2):
                S[h, pl.ds(y0 * 8 + m, YC, stride=8), :] = val[:, 128 * h : 128 * h + 128]
        a0, a1, b0, b1, p0, p1 = carry
        for i in range(YC):
            f0 = S[0, pl.ds(y0 * 8 + 8 * i, 8), :]
            f1 = S[1, pl.ds(y0 * 8 + 8 * i, 8), :]
            a0, a1 = f0 + rate[0] * a0, f1 + rate[1] * a1
            b0, b1 = b0 + p0 * f0, b1 + p1 * f1
            p0, p1 = p0 * rate[0], p1 * rate[1]
        return a0, a1, b0, b1, p0, p1

    zero = jnp.zeros((8, 128), f32)
    one = jnp.ones((8, 128), f32)
    a0, a1, b0, b1, p0, p1 = lax.fori_loop(0, chunks, x_forward, (zero, zero, zero, zero, one, one))

    half = 16
    for h, (a, b, p) in enumerate([(a0, b0, p0), (a1, b1, p1)]):
        for j in range(8):
            IFS[h * 8 + j] = a[j : j + 1, :]
            IFS[half + h * 8 + j] = b[j : j + 1, :]
            RP[h * 8 + j] = p[j : j + 1, :]
    IFR[0] = IFS[gy]

    @pl.loop(1, ny_dev)
    def _(t):
        i = py(t)
        slot = (ny_dev - t) + (i // half) * (2 * t - ny_dev)
        send(IFS.at[i], IFR.at[slot], is_sem.at[0], ir_sem.at[0], {"gy": i}).start()

    others = pl.ds(1, ny_dev - 1)
    send(IFS.at[others], IFR.at[others], is_sem.at[0], ir_sem.at[0], {"gy": py(1)}).wait()
    acc = IFR[...]
    power = RP[lax.rem(gy, half)][None]
    step = 1
    while step < ny_dev:
        acc = acc + power * jnp.concatenate([acc[ny_dev - step :], acc[: ny_dev - step]], axis=0)
        power = power * power
        step *= 2
    acc = acc * (1.0 / (1.0 - power))
    IFO[...] = jnp.concatenate([acc[ny_dev - 1 :], acc[: ny_dev - 1]], axis=0)
    IFB[gy] = IFO[0]
    sign = 1 - 2 * (gy // half)

    @pl.loop(1, ny_dev)
    def _(t):
        dev = lax.rem(gy + t * sign + ny_dev, ny_dev)
        send(IFO.at[t], IFB.at[gy], is_sem.at[1], ir_sem.at[1], {"gy": dev}).start()

    send(IFO.at[others], IFB.at[others], is_sem.at[1], ir_sem.at[1], {"gy": py(1)}).wait()
    ain = [jnp.concatenate([IFB[h * 8 + j] for j in range(8)], axis=0) for h in range(2)]
    bin_ = [jnp.concatenate([IFB[half + h * 8 + j] for j in range(8)], axis=0) for h in range(2)]

    def back(i, carry):
        y = ny - 1 - i
        at = pl.ds(pl.multiple_of(y * 8, 8), 8)
        out = []
        for h in range(2):
            b = S[h, at, :] + rate[h] * carry[h]
            SB[h, at, :] = rate[h] * carry[h]
            out.append(b)
        return tuple(out)

    lax.fori_loop(0, ny, back, tuple(bin_), unroll=8)

    def forth(y, carry):
        at = pl.ds(pl.multiple_of(y * 8, 8), 8)
        out = []
        for h in range(2):
            a = S[h, at, :] + rate[h] * carry[h]
            S[h, at, :] = scale[h] * (a + SB[h, at, :])
            out.append(a)
        return tuple(out)

    last = lax.fori_loop(0, ny, forth, tuple(ain), unroll=8)
    for h in range(2):
        S[h, ny * 8 : ny * 8 + 8, :] = scale[h] * (rate[h] * last[h] + bin_[h])
        S[h, ny * 8 + 8 : ny * 8 + 64, :] = jnp.zeros((56, 128), f32)

    def x_inverse(y0, n, put):
        for m in range(8):
            for h in range(2):
                Z[m * n : m * n + n, 128 * h : 128 * h + 128] = S[h, pl.ds(y0 * 8 + m, n, stride=8), :]
        o0 = dot3(Z[0:n, :], MATS[6], MATS[7])
        om = dot3(Z[n : 8 * n, :], MATS[4], MATS[5])
        Z[0:n, :] = o0
        Z[n : 8 * n, :] = om
        for i in range(n // 8):
            zr, zi = {}, {}
            for m in range(1, 8):
                co, si = tab_ref[m : m + 1, :], tab_ref[8 + m : 9 + m, :]
                at = m * n + 8 * i
                a, b = Z[at : at + 8, 0:128], Z[at : at + 8, 128:256]
                zr[m] = a * co - b * si
                zi[m] = a * si + b * co
            put(i, inv16(Z[8 * i : 8 * i + 8, 0:128], Z[8 * i : 8 * i + 8, 128:256], zr, zi))

    lane_8 = lanes((8, 128))

    @pl.loop(0, chunks)
    def _(c):
        y0 = pl.multiple_of(c * YC, YC)

        def put(i, x):
            edge = jnp.zeros((8, 128), f32)
            for q in range(16):
                TX2[q // 2, c, q % 2, 8 * i : 8 * i + 8, :] = x[q]
            for d in range(nx_dev):
                edge = jnp.where(lane_8 == d, roll(x[(2 * d + 2) % 16], d, 1), edge)
            EW[pl.ds(y0 + 8 * i, 8), :] = edge

        x_inverse(y0, YC, put)
        pltpu.make_async_copy(TX2.at[gx, c], RX2.at[c, gx], l2_sem.at[c]).start()
        for t in range(1, nx_dev):
            g = px(t)
            send(TX2.at[g, c], RX2.at[c, gx], s2_sem.at[c, t], r2_sem.at[c, gx], {"gx": g}).start()

    EW[ny:128, :] = jnp.zeros((128 - ny, 128), f32)
    ewt = jnp.transpose(EW[...])
    row8 = rows_of((8, 128))

    def put_north(i, x):
        for d in range(nx_dev):
            e = jnp.broadcast_to(ewt[d : d + 1, :], (8, 128))
            n0 = jnp.broadcast_to(x[2 * d][0:1], (8, 128))
            n1 = jnp.broadcast_to(x[2 * d + 1][0:1], (8, 128))
            X2[d] = jnp.where(row8 == 0, n0, jnp.where(row8 == 1, n1, e))

    x_inverse(ny, 8, put_north)
    pltpu.make_async_copy(X2.at[gx], XR.at[gx], l2_sem.at[chunks]).start()
    for t in range(1, nx_dev):
        g = px(t)
        send(X2.at[g], XR.at[gx], sx_sem.at[t], rx_sem.at[gx], {"gx": g}).start()

    @pl.loop(0, chunks)
    def _(c):
        cen = pl.ds(pl.multiple_of(c * YC, YC), YC)
        pltpu.make_async_copy(TX2.at[gx, c], RX2.at[c, gx], l2_sem.at[c]).wait()
        for t in range(1, nx_dev):
            g = px(t)
            send(TX2.at[g, c], RX2.at[c, g], s2_sem.at[c, t], r2_sem.at[c, g], {"gx": g}).wait_recv()
        for h in range(2):
            col = [RX2[c, j, h] for j in range(levels)]
            for k in range(levels):
                acc = TI[k : k + 1, :] * col[0]
                for j in range(1, levels):
                    acc = acc + TI[j * 8 + k : j * 8 + k + 1, :] * col[j]
                p_ref[k, cen, 128 * h : 128 * h + 128] = acc

    pltpu.make_async_copy(X2.at[gx], XR.at[gx], l2_sem.at[chunks]).wait()
    for t in range(1, nx_dev):
        g = px(t)
        send(X2.at[g], XR.at[g], sx_sem.at[t], rx_sem.at[g], {"gx": g}).wait_recv()
    east = jnp.zeros((8, 128), f32)
    for k in range(levels):
        acc = TI[k : k + 1, :] * XR[0]
        for j in range(1, levels):
            acc = acc + TI[j * 8 + k : j * 8 + k + 1, :] * XR[j]
        EX[k] = acc
        east = jnp.where(row8 == k, jnp.broadcast_to(acc[2:3, :], (8, 128)), east)
    EC[0:8, :] = east
    EC[8:128, :] = jnp.zeros((120, 128), f32)
    EC[...] = jnp.transpose(EC[...])

    @pl.loop(0, levels)
    def _(k):
        p = p_ref[k]
        pleft, pright = p[:, :128], p[:, 128:]
        ec = EC[0:ny, :]
        col = jnp.sum(jnp.where(lane_n == k, ec, 0.0), axis=1, keepdims=True)
        a, b = roll(pleft, -1, 1), roll(pright, -1, 1)
        gl = jnp.where(lane_n < 127, a, b) - pleft
        gr = jnp.where(lane_n < 127, b, jnp.broadcast_to(col, (ny, 128))) - pright
        un_ref[k] = U[k] - DT * jnp.concatenate([gl, gr], axis=1)
        ex = EX[k]
        north = jnp.concatenate([ex[0:1, :], ex[1:2, :]], axis=1)
        shifted = roll(p, -1, 0)
        shifted = jnp.where(rows_of((ny, nx)) < ny - 1, shifted, jnp.broadcast_to(north, (ny, nx)))
        vn_ref[k] = V[k, mid, :] - DT * (shifted - p)

    for k in range(levels):
        g = COEF[48 + k : 49 + k, :]
        if k + 1 < levels:
            wn_ref[k] = WS[k] - g * (p_ref[k + 1] - p_ref[k])
        else:
            wn_ref[k] = WS[k] + g * p_ref[k]

    @pl.loop(0, chunks)
    def _(c):
        for t in range(1, nx_dev):
            g = px(t)
            send(TX1.at[g, c], RX1.at[c, g], s1_sem.at[c, t], r1_sem.at[c, g], {"gx": g}).wait_send()
            send(TX2.at[g, c], RX2.at[c, g], s2_sem.at[c, t], r2_sem.at[c, g], {"gx": g}).wait_send()

    for t in range(1, nx_dev):
        g = px(t)
        send(X2.at[g], XR.at[g], sx_sem.at[t], rx_sem.at[g], {"gx": g}).wait_send()


def per_device(u_face, v_face, w_face, theta_field, density, thickness):
    nx_dev = lax.axis_size("gx")
    ny_dev = lax.axis_size("gy")
    levels, ny, nx = u_face.shape
    chunks = ny // YC
    mats, tab = tables()
    vm = pltpu.VMEM
    dma = pltpu.SemaphoreType.DMA
    out = jax.ShapeDtypeStruct(u_face.shape, f32)
    any_ = pl.BlockSpec(memory_space=pl.ANY)
    smem = pl.BlockSpec(memory_space=pltpu.SMEM)
    vmem = pl.BlockSpec(memory_space=pltpu.VMEM)
    scratch = [
        vm((levels, ny, nx), f32),
        vm((levels, ny + 8, nx), f32),
        vm((levels, ny + 16, nx), f32),
        vm((levels, ny + 16, nx), f32),
        vm((8, 256, 256), bf16),
        vm((56, 256), f32),
        vm((64, 128), f32),
        vm((64, 128), f32),
        vm((8, 8, 128), f32),
        vm((ny, 128), f32), vm((ny, 128), f32), vm((ny, 128), f32), vm((ny, 128), f32),
        vm((levels, 8, nx), f32), vm((levels, 8, nx), f32),
        vm((levels, 8, nx), f32), vm((levels, 8, nx), f32),
        vm((ny, 128), f32),
        vm((levels, 8, nx), f32),
        vm((levels, ny, nx), f32),
        vm((levels, YC, nx), f32),
        vm((levels, chunks, 2, YC, 128), f32),
        vm((chunks, nx_dev, 2, YC, 128), f32),
        vm((8 * YC, 256), f32),
        vm((2, (ny + 8) * 8, 128), f32),
        vm((2, ny * 8, 128), f32),
        vm((32, 1, 128), f32), vm((32, 1, 128), f32), vm((32, 1, 128), f32), vm((32, 1, 128), f32),
        vm((16, 1, 128), f32),
        vm((nx_dev, chunks, 2, YC, 128), f32),
        vm((chunks, levels, 2, YC, 128), f32),
        vm((nx_dev, 8, 128), f32),
        vm((levels, 8, 128), f32),
        vm((128, 128), f32),
        vm((128, 128), f32),
        vm((levels, 8, 128), f32),
        dma((5,)), dma((4,)), dma((4,)),
        dma((chunks, nx_dev)), dma((chunks, nx_dev)), dma((chunks,)),
        dma((2,)), dma((2,)),
        dma((chunks, nx_dev)), dma((chunks, nx_dev)), dma((chunks + 1,)),
        dma((nx_dev,)), dma((nx_dev,)),
    ]
    return pl.pallas_call(
        functools.partial(kernel, nx_dev, ny_dev),
        out_shape=(out,) * 5,
        in_specs=[smem, smem, vmem, any_, any_, any_, any_, any_],
        out_specs=(vmem,) * 5,
        scratch_shapes=scratch,
        compiler_params=pltpu.CompilerParams(
            collective_id=0, has_side_effects=True, vmem_limit_bytes=40 << 20
        ),
        name="substep",
    )(density, thickness, jnp.asarray(tab), u_face, v_face, w_face, theta_field, jnp.asarray(mats))


def solution(mesh):
    spec = P(None, "gy", "gx")
    return jax.shard_map(
        per_device,
        mesh=mesh,
        in_specs=(spec, spec, spec, spec, P(), P()),
        out_specs=(spec,) * 5,
        check_vma=False,
    )
```

profile of v0, /device:TPU:1, one launch (start us, length us, event | category | flops | bytes accessed | tf_op | source)
XLA Modules:
  0.0 62.1 jit_solution(10020622862312847620)
XLA Ops:
  0.6 0.0 copy-start
  0.6 1.2 %copy-done = bf16[8,256,256]{2,1,0:T(8,128)(2,1)S(1)} copy-done((bf16[8,256,256]{2,1,0:T(8,128)(2,1)S(1)}, bf16[8,256,256]{2,1,0:T(8,128)(2,1)}, u32[]{:S(2)}) %copy-start) | copy-done | bytes 1048600
  1.9 0.0 copy-start.1
  1.9 1.0 %copy-done.1 = f32[8,64,256]{2,1,0:T(8,128)S(1)} copy-done((f32[8,64,256]{2,1,0:T(8,128)S(1)}, f32[8,64,256]{2,1,0:T(8,128)}, u32[]{:S(2)}) %copy-start.1) | copy-done | bytes 524312
  2.9 0.0 copy-start.2
  2.9 1.0 %copy-done.2 = f32[8,64,256]{2,1,0:T(8,128)S(1)} copy-done((f32[8,64,256]{2,1,0:T(8,128)S(1)}, f32[8,64,256]{2,1,0:T(8,128)}, u32[]{:S(2)}) %copy-start.2) | copy-done | bytes 524312
  3.9 0.0 copy-start.3
  3.9 1.0 %copy-done.3 = f32[8,64,256]{2,1,0:T(8,128)S(1)} copy-done((f32[8,64,256]{2,1,0:T(8,128)S(1)}, f32[8,64,256]{2,1,0:T(8,128)}, u32[]{:S(2)}) %copy-start.3) | copy-done | bytes 524312
  5.0 0.0 copy-start.4
  5.0 1.0 %copy-done.4 = f32[8,64,256]{2,1,0:T(8,128)S(1)} copy-done((f32[8,64,256]{2,1,0:T(8,128)S(1)}, f32[8,64,256]{2,1,0:T(8,128)}, u32[]{:S(2)}) %copy-start.4) | copy-done | bytes 524312
  6.0 0.0 copy-start.5
  6.0 0.7 %copy-done.5 = f32[32,128]{1,0:T(8,128)S(1)} copy-done((f32[32,128]{1,0:T(8,128)S(1)}, f32[32,128]{1,0:T(8,128)}, u32[]{:S(2)}) %copy-start.5) | copy-done | bytes 16408
  6.7 0.0 copy-start.6
  6.8 0.7 %copy-done.6 = f32[8]{0:T(128)S(1)} copy-done((f32[8]{0:T(128)S(1)}, f32[8]{0:T(128)}, u32[]{:S(2)}) %copy-start.6) | copy-done | bytes 56
  7.4 0.0 copy-start.7
  7.4 0.7 %copy-done.7 = f32[8]{0:T(128)S(1)} copy-done((f32[8]{0:T(128)S(1)}, f32[8]{0:T(128)}, u32[]{:S(2)}) %copy-start.7) | copy-done | bytes 56
  8.1 50.0 %substep.1 = (f32[8,64,256]{2,1,0:T(8,128)S(1)}, f32[8,64,256]{2,1,0:T(8,128)S(1)}, f32[8,64,256]{2,1,0:T(8,128)S(1)}, f32[8,64,256]{2,1,0:T(8,128)S(1)}, f32[8,64,256]{2,1,0:T(8,128)S(1)}) custom-call(f32[8]{0:T(128)S(1)} %copy-done.6, f32[8]{0:T(128)S(1)} %copy-done.7, f32[32,128]{1,0:T(8,128)S(1)} %copy-done.5, f32[8,64,256]{2,1,0:T(8,128)S(1)} %copy-done.1, ...), custom_call_target="tpu_custom_call" | custom-call | tf_op jit(solution)/shard_map/substep/pallas_call | solution.py:694
  58.1 0.8 %copy.18 = f32[8,64,256]{2,1,0:T(8,128)} copy(f32[8,64,256]{2,1,0:T(8,128)S(1)} %get-tuple-element.10) | data formatting | bytes 1048576
  58.9 0.8 %copy.19 = f32[8,64,256]{2,1,0:T(8,128)} copy(f32[8,64,256]{2,1,0:T(8,128)S(1)} %get-tuple-element.11) | data formatting | bytes 1048576
  59.7 0.8 %copy.20 = f32[8,64,256]{2,1,0:T(8,128)} copy(f32[8,64,256]{2,1,0:T(8,128)S(1)} %get-tuple-element.12) | data formatting | bytes 1048576
  60.5 0.8 %copy.21 = f32[8,64,256]{2,1,0:T(8,128)} copy(f32[8,64,256]{2,1,0:T(8,128)S(1)} %get-tuple-element.13) | data formatting | bytes 1048576
  61.3 0.8 %copy.22 = f32[8,64,256]{2,1,0:T(8,128)} copy(f32[8,64,256]{2,1,0:T(8,128)S(1)} %get-tuple-element.14) | data formatting | bytes 1048576
Async XLA Ops:
  0.6 1.2 %copy-start = (bf16[8,256,256]{2,1,0:T(8,128)(2,1)S(1)}, bf16[8,256,256]{2,1,0:T(8,128)(2,1)}, u32[]{:S(2)}) copy-start(bf16[8,256,256]{2,1,0:T(8,128)(2,1)} %constant.5.clone.mats_hbm) | copy-start | bytes 3145732
  1.9 1.0 %copy-start.1 = (f32[8,64,256]{2,1,0:T(8,128)S(1)}, f32[8,64,256]{2,1,0:T(8,128)}, u32[]{:S(2)}) copy-start(f32[8,64,256]{2,1,0:T(8,128)} %u_hbm.1) | copy-start | bytes 1572868
  2.9 1.0 %copy-start.2 = (f32[8,64,256]{2,1,0:T(8,128)S(1)}, f32[8,64,256]{2,1,0:T(8,128)}, u32[]{:S(2)}) copy-start(f32[8,64,256]{2,1,0:T(8,128)} %v_hbm.1) | copy-start | bytes 1572868
  3.9 1.0 %copy-start.3 = (f32[8,64,256]{2,1,0:T(8,128)S(1)}, f32[8,64,256]{2,1,0:T(8,128)}, u32[]{:S(2)}) copy-start(f32[8,64,256]{2,1,0:T(8,128)} %w_hbm.1) | copy-start | bytes 1572868
  5.0 1.0 %copy-start.4 = (f32[8,64,256]{2,1,0:T(8,128)S(1)}, f32[8,64,256]{2,1,0:T(8,128)}, u32[]{:S(2)}) copy-start(f32[8,64,256]{2,1,0:T(8,128)} %th_hbm.1) | copy-start | bytes 1572868
  6.0 0.7 %copy-start.5 = (f32[32,128]{1,0:T(8,128)S(1)}, f32[32,128]{1,0:T(8,128)}, u32[]{:S(2)}) copy-start(f32[32,128]{1,0:T(8,128)} %constant.4.clone.tab_ref) | copy-start | bytes 49156
  6.7 0.7 %copy-start.6 = (f32[8]{0:T(128)S(1)}, f32[8]{0:T(128)}, u32[]{:S(2)}) copy-start(f32[8]{0:T(128)} %den_ref.1) | copy-start | bytes 100
  7.4 0.7 %copy-start.7 = (f32[8]{0:T(128)S(1)}, f32[8]{0:T(128)}, u32[]{:S(2)}) copy-start(f32[8]{0:T(128)} %thk_ref.1) | copy-start | bytes 100
where the time goes:
time: 62.5 us; the launch traced here: 62.1 us
  Pallas kernels  50 us (80%)
  local copies, waits for them, and re-layouts  11.4 us (18%)
  between operations  0.66 us (1%)
    pallas_call x1, Pallas kernels, per_device(): pl.pallas_call(functools.partial(kernel, nx_dev, ny_dev), out_shape=(out,...  50 us
    unnamed x21, local copies, waits for them, and re-layouts  11.4 us

commit v1 on v0

--- a/solution.py
+++ b/solution.py
@@ -127,11 +127,11 @@
 
 def kernel(
     nx_dev, ny_dev,
-    den_ref, thk_ref, tab_ref, u_hbm, v_hbm, w_hbm, th_hbm, mats_hbm,
-    un_ref, vn_ref, wn_ref, tn_ref, p_ref,
-    U, V, W, TH, MATS, COEF, TF, TI, LAM,
+    den_hbm, thk_hbm, tab_hbm, u_hbm, v_hbm, w_hbm, th_hbm, mats_hbm,
+    U, V, WS, tn_ref, RX2, XR, TI, COEF,
+    den_ref, thk_ref, tab_ref, W, TH, MATS, TF, LAM,
     PE_S, PW_S, PE_R, PW_R, YN_S, YS_S, YN_R, YS_R, FPK, FYP,
-    WS, SRC, TX1, RX1, Z, S, SB, IFS, IFR, IFO, IFB, RP, TX2, RX2, X2, XR, EW, EC, EX,
+    SRC, TX1, RX1, Z, S, SB, IFS, IFR, IFO, IFB, RP, TX2, X2, EW,
     in_sem, hs_sem, hr_sem, s1_sem, r1_sem, l1_sem, is_sem, ir_sem, s2_sem, r2_sem, l2_sem,
     sx_sem, rx_sem,
 ):
@@ -147,6 +147,11 @@
         return lax.rem(gy + t, ny_dev)
 
     mid = pl.ds(8, ny)
+    small = [
+        pltpu.make_async_copy(den_hbm, den_ref, in_sem.at[5]),
+        pltpu.make_async_copy(thk_hbm, thk_ref, in_sem.at[6]),
+        pltpu.make_async_copy(tab_hbm, tab_ref, in_sem.at[7]),
+    ]
     loads = [
         pltpu.make_async_copy(w_hbm, W.at[:, mid, :], in_sem.at[0]),
         pltpu.make_async_copy(th_hbm, TH.at[:, mid, :], in_sem.at[1]),
@@ -154,7 +159,7 @@
         pltpu.make_async_copy(v_hbm, V.at[:, mid, :], in_sem.at[3]),
         pltpu.make_async_copy(mats_hbm, MATS, in_sem.at[4]),
     ]
-    for cp in loads:
+    for cp in small + loads:
         cp.start()
 
     barrier = pltpu.get_barrier_semaphore()
@@ -164,6 +169,9 @@
     @pl.loop(1, ny_dev)
     def _(t):
         pl.semaphore_signal(barrier, inc=1, device_id={"gy": py(t)}, device_id_type=MESH)
+
+    for cp in small:
+        cp.wait()
 
     r8 = rows_of((8, 128))
     j8 = lax.rem(lanes((8, 128)), 8)
@@ -579,11 +587,42 @@
 
     @pl.loop(0, chunks)
     def _(c):
-        cen = pl.ds(pl.multiple_of(c * YC, YC), YC)
         pltpu.make_async_copy(TX2.at[gx, c], RX2.at[c, gx], l2_sem.at[c]).wait()
         for t in range(1, nx_dev):
             g = px(t)
             send(TX2.at[g, c], RX2.at[c, g], s2_sem.at[c, t], r2_sem.at[c, g], {"gx": g}).wait_recv()
+
+    pltpu.make_async_copy(X2.at[gx], XR.at[gx], l2_sem.at[chunks]).wait()
+    for t in range(1, nx_dev):
+        g = px(t)
+        send(X2.at[g], XR.at[g], sx_sem.at[t], rx_sem.at[g], {"gx": g}).wait_recv()
+
+    @pl.loop(0, chunks)
+    def _(c):
+        for t in range(1, nx_dev):
+            g = px(t)
+            send(TX1.at[g, c], RX1.at[c, g], s1_sem.at[c, t], r1_sem.at[c, g], {"gx": g}).wait_send()
+            send(TX2.at[g, c], RX2.at[c, g], s2_sem.at[c, t], r2_sem.at[c, g], {"gx": g}).wait_send()
+
+    for t in range(1, nx_dev):
+        g = px(t)
+        send(X2.at[g], XR.at[g], sx_sem.at[t], rx_sem.at[g], {"gx": g}).wait_send()
+
+
+def finish(
+    U, V, WS, tn_ref, RX2, XR, TI, COEF, un_hbm, vn_hbm, wn_hbm, tn_hbm, p_hbm,
+    un_ref, vn_ref, wn_ref, p_ref, EC, EX, tn_sem, out_sem,
+):
+    levels, ny, nx = U.shape
+    chunks = ny // YC
+    theta = pltpu.make_async_copy(tn_ref, tn_hbm, tn_sem.at[0])
+    theta.start()
+    lane_n = lanes((ny, 128))
+    row8 = rows_of((8, 128))
+
+    @pl.loop(0, chunks)
+    def _(c):
+        cen = pl.ds(pl.multiple_of(c * YC, YC), YC)
         for h in range(2):
             col = [RX2[c, j, h] for j in range(levels)]
             for k in range(levels):
@@ -592,10 +631,13 @@
                     acc = acc + TI[j * 8 + k : j * 8 + k + 1, :] * col[j]
                 p_ref[k, cen, 128 * h : 128 * h + 128] = acc
 
-    pltpu.make_async_copy(X2.at[gx], XR.at[gx], l2_sem.at[chunks]).wait()
-    for t in range(1, nx_dev):
-        g = px(t)
-        send(X2.at[g], XR.at[g], sx_sem.at[t], rx_sem.at[g], {"gx": g}).wait_recv()
+    def out(i, ref, hbm, k):
+        return pltpu.make_async_copy(ref.at[k], hbm.at[k], out_sem.at[i, k])
+
+    outs = [(p_ref, p_hbm), (un_ref, un_hbm), (vn_ref, vn_hbm), (wn_ref, wn_hbm)]
+    for k in range(levels):
+        out(0, p_ref, p_hbm, k).start()
+
     east = jnp.zeros((8, 128), f32)
     for k in range(levels):
         acc = TI[k : k + 1, :] * XR[0]
@@ -607,39 +649,32 @@
     EC[8:128, :] = jnp.zeros((120, 128), f32)
     EC[...] = jnp.transpose(EC[...])
 
-    @pl.loop(0, levels)
-    def _(k):
+    for k in range(levels):
         p = p_ref[k]
         pleft, pright = p[:, :128], p[:, 128:]
-        ec = EC[0:ny, :]
-        col = jnp.sum(jnp.where(lane_n == k, ec, 0.0), axis=1, keepdims=True)
+        col = jnp.broadcast_to(EC[0:ny, k : k + 1], (ny, 128))
         a, b = roll(pleft, -1, 1), roll(pright, -1, 1)
         gl = jnp.where(lane_n < 127, a, b) - pleft
-        gr = jnp.where(lane_n < 127, b, jnp.broadcast_to(col, (ny, 128))) - pright
+        gr = jnp.where(lane_n < 127, b, col) - pright
         un_ref[k] = U[k] - DT * jnp.concatenate([gl, gr], axis=1)
+        out(1, un_ref, un_hbm, k).start()
         ex = EX[k]
         north = jnp.concatenate([ex[0:1, :], ex[1:2, :]], axis=1)
         shifted = roll(p, -1, 0)
         shifted = jnp.where(rows_of((ny, nx)) < ny - 1, shifted, jnp.broadcast_to(north, (ny, nx)))
-        vn_ref[k] = V[k, mid, :] - DT * (shifted - p)
-
-    for k in range(levels):
+        vn_ref[k] = V[k, 8 : 8 + ny, :] - DT * (shifted - p)
+        out(2, vn_ref, vn_hbm, k).start()
         g = COEF[48 + k : 49 + k, :]
         if k + 1 < levels:
-            wn_ref[k] = WS[k] - g * (p_ref[k + 1] - p_ref[k])
+            wn_ref[k] = WS[k] - g * (p_ref[k + 1] - p)
         else:
-            wn_ref[k] = WS[k] + g * p_ref[k]
-
-    @pl.loop(0, chunks)
-    def _(c):
-        for t in range(1, nx_dev):
-            g = px(t)
-            send(TX1.at[g, c], RX1.at[c, g], s1_sem.at[c, t], r1_sem.at[c, g], {"gx": g}).wait_send()
-            send(TX2.at[g, c], RX2.at[c, g], s2_sem.at[c, t], r2_sem.at[c, g], {"gx": g}).wait_send()
-
-    for t in range(1, nx_dev):
-        g = px(t)
-        send(X2.at[g], XR.at[g], sx_sem.at[t], rx_sem.at[g], {"gx": g}).wait_send()
+            wn_ref[k] = WS[k] + g * p
+        out(3, wn_ref, wn_hbm, k).start()
+
+    theta.wait()
+    for k in range(levels):
+        for i, (ref, hbm) in enumerate(outs):
+            out(i, ref, hbm, k).wait()
 
 
 def per_device(u_face, v_face, w_face, theta_field, density, thickness):
@@ -650,18 +685,15 @@
     mats, tab = tables()
     vm = pltpu.VMEM
     dma = pltpu.SemaphoreType.DMA
-    out = jax.ShapeDtypeStruct(u_face.shape, f32)
-    any_ = pl.BlockSpec(memory_space=pl.ANY)
-    smem = pl.BlockSpec(memory_space=pltpu.SMEM)
+    full = (levels, ny, nx)
+    out = jax.ShapeDtypeStruct(full, f32)
+    hbm = pl.BlockSpec(memory_space=pltpu.HBM)
     vmem = pl.BlockSpec(memory_space=pltpu.VMEM)
     scratch = [
-        vm((levels, ny, nx), f32),
-        vm((levels, ny + 8, nx), f32),
+        pltpu.SMEM((levels,), f32), pltpu.SMEM((levels,), f32), vm((32, 128), f32),
         vm((levels, ny + 16, nx), f32),
         vm((levels, ny + 16, nx), f32),
         vm((8, 256, 256), bf16),
-        vm((56, 256), f32),
-        vm((64, 128), f32),
         vm((64, 128), f32),
         vm((8, 8, 128), f32),
         vm((ny, 128), f32), vm((ny, 128), f32), vm((ny, 128), f32), vm((ny, 128), f32),
@@ -669,7 +701,6 @@
         vm((levels, 8, nx), f32), vm((levels, 8, nx), f32),
         vm((ny, 128), f32),
         vm((levels, 8, nx), f32),
-        vm((levels, ny, nx), f32),
         vm((levels, YC, nx), f32),
         vm((levels, chunks, 2, YC, 128), f32),
         vm((chunks, nx_dev, 2, YC, 128), f32),
@@ -679,29 +710,49 @@
         vm((32, 1, 128), f32), vm((32, 1, 128), f32), vm((32, 1, 128), f32), vm((32, 1, 128), f32),
         vm((16, 1, 128), f32),
         vm((nx_dev, chunks, 2, YC, 128), f32),
-        vm((chunks, levels, 2, YC, 128), f32),
         vm((nx_dev, 8, 128), f32),
-        vm((levels, 8, 128), f32),
         vm((128, 128), f32),
-        vm((128, 128), f32),
-        vm((levels, 8, 128), f32),
-        dma((5,)), dma((4,)), dma((4,)),
+        dma((8,)), dma((4,)), dma((4,)),
         dma((chunks, nx_dev)), dma((chunks, nx_dev)), dma((chunks,)),
         dma((2,)), dma((2,)),
         dma((chunks, nx_dev)), dma((chunks, nx_dev)), dma((chunks + 1,)),
         dma((nx_dev,)), dma((nx_dev,)),
     ]
-    return pl.pallas_call(
+    mid = pl.pallas_call(
         functools.partial(kernel, nx_dev, ny_dev),
-        out_shape=(out,) * 5,
-        in_specs=[smem, smem, vmem, any_, any_, any_, any_, any_],
-        out_specs=(vmem,) * 5,
+        out_shape=(
+            out,
+            jax.ShapeDtypeStruct((levels, ny + 8, nx), f32),
+            out,
+            out,
+            jax.ShapeDtypeStruct((chunks, levels, 2, YC, 128), f32),
+            jax.ShapeDtypeStruct((levels, 8, 128), f32),
+            jax.ShapeDtypeStruct((64, 128), f32),
+            jax.ShapeDtypeStruct((56, 256), f32),
+        ),
+        in_specs=[hbm] * 8,
+        out_specs=(vmem,) * 8,
         scratch_shapes=scratch,
         compiler_params=pltpu.CompilerParams(
-            collective_id=0, has_side_effects=True, vmem_limit_bytes=40 << 20
+            collective_id=0, has_side_effects=True, vmem_limit_bytes=36 << 20
         ),
         name="substep",
-    )(density, thickness, jnp.asarray(tab), u_face, v_face, w_face, theta_field, jnp.asarray(mats))
+    )(*(
+        pltpu.with_memory_space_constraint(a, pltpu.HBM)
+        for a in (density, thickness, jnp.asarray(tab), u_face, v_face, w_face, theta_field, jnp.asarray(mats))
+    ))
+    return pl.pallas_call(
+        finish,
+        out_shape=(out,) * 5,
+        in_specs=[vmem] * 8,
+        out_specs=(hbm,) * 5,
+        scratch_shapes=[
+            vm(full, f32), vm(full, f32), vm(full, f32), vm(full, f32),
+            vm((128, 128), f32), vm((levels, 8, 128), f32), dma((1,)), dma((4, levels)),
+        ],
+        compiler_params=pltpu.CompilerParams(vmem_limit_bytes=24 << 20),
+        name="finish",
+    )(*mid)
 
 
 def solution(mesh):

time: 62.5 us -> 51.1 us (0.82)
  local copies, waits for them, and re-layouts: 11.4 us -> 0 us
    unnamed x21 -> x0, local copies, waits for them, and re-layouts: 11.4 us -> none
    pallas_call x0 -> x1, Pallas kernels: none -> 1.92 us  [per_device(): pl.pallas_call(finish, out_shape=(out,) * 5, in_specs=[vmem] * 8, out_spe...]
    pallas_call x1, Pallas kernels: 50 us -> 48.4 us  [per_device(): pl.pallas_call(functools.partial(kernel, nx_dev, ny_dev), out_shape=(out,...]
where the time goes in v1:
time: 51.1 us; the launch traced here: 51 us
  Pallas kernels  50.3 us (98%)
  between operations  0.64 us (1%)
    pallas_call x1, Pallas kernels, per_device(): pl.pallas_call(functools.partial(kernel, nx_dev, ny_dev), out_shape=(out,...  48.4 us
    pallas_call x1, Pallas kernels, per_device(): pl.pallas_call(finish, out_shape=(out,) * 5, in_specs=[vmem] * 8, out_spe...  1.92 us

profile of v1, /device:TPU:1, one launch (start us, length us, event | category | flops | bytes accessed | tf_op | source)
XLA Modules:
  0.0 51.0 jit_solution(14517009486949649924)
XLA Ops:
  0.6 48.4 %substep.1 = (f32[8,64,256]{2,1,0:T(8,128)S(1)}, f32[8,72,256]{2,1,0:T(8,128)S(1)}, f32[8,64,256]{2,1,0:T(8,128)S(1)}, f32[8,64,256]{2,1,0:T(8,128)S(1)}, f32[4,...) custom-call(f32[8]{0:T(128)} %den_hbm.1, f32[8]{0:T(128)} %thk_hbm.1, ...), custom_call_target="tpu_custom_call" | custom-call | tf_op jit(solution)/shard_map/substep/pallas_call | solution.py:721
  49.1 1.9 %finish.1 = (f32[8,64,256]{2,1,0:T(8,128)}, f32[8,64,256]{2,1,0:T(8,128)}, f32[8,64,256]{2,1,0:T(8,128)}, f32[8,64,256]{2,1,0:T(8,128)}, f32[8,64,256]{2,1,0:T(8,128)}) custom-call(f32[8,64,256]{2,1,0:T(8,128)S(1)} %get-tuple-element.13.U, f32[8,72,256]{2,1,0:T(8,128)S(1)} %get-tuple-element.14.V, f32[8,64,256]{2,1,0:T(8,128)S(1)} %get-tuple-element.15.WS, ...), custom_call_target="tpu_custom_call" | custom-call | tf_op jit(solution)/shard_map/finish/pallas_call | solution.py:744

commit v2 on v1

--- a/solution.py
+++ b/solution.py
@@ -128,12 +128,12 @@
 def kernel(
     nx_dev, ny_dev,
     den_hbm, thk_hbm, tab_hbm, u_hbm, v_hbm, w_hbm, th_hbm, mats_hbm,
-    U, V, WS, tn_ref, RX2, XR, TI, COEF,
+    U, V, WS, tn_ref, p_ref, XR, TI, COEF,
     den_ref, thk_ref, tab_ref, W, TH, MATS, TF, LAM,
     PE_S, PW_S, PE_R, PW_R, YN_S, YS_S, YN_R, YS_R, FPK, FYP,
-    SRC, TX1, RX1, Z, S, SB, IFS, IFR, IFO, IFB, RP, TX2, X2, EW,
+    SRC, TX1, RX1, Z, S, SA, SB, PWR, IFS, IFR, CBS, CBR, INS, INR, TX2, RX2, X2, EW,
     in_sem, hs_sem, hr_sem, s1_sem, r1_sem, l1_sem, is_sem, ir_sem, s2_sem, r2_sem, l2_sem,
-    sx_sem, rx_sem,
+    sx_sem, rx_sem, near_sem,
 ):
     gx = lax.axis_index("gx")
     gy = lax.axis_index("gy")
@@ -145,6 +145,19 @@
 
     def py(t):
         return lax.rem(gy + t, ny_dev)
+
+    n_chips = ny_dev // 2
+    chip, core = gy // 2, lax.rem(gy, 2)
+
+    def chip_at(t):
+        return 2 * lax.rem(chip + t, n_chips) + core
+
+    def greet(stage):
+        for t in (2**stage, n_chips - 2**stage):
+            pl.semaphore_signal(near_sem.at[stage], inc=1, device_id={"gy": chip_at(t)}, device_id_type=MESH)
+
+    def greeted(stage):
+        pl.semaphore_wait(near_sem.at[stage], 2)
 
     mid = pl.ds(8, ny)
     small = [
@@ -166,81 +179,10 @@
     for t in range(1, nx_dev):
         pl.semaphore_signal(barrier, inc=1, device_id={"gx": px(t)}, device_id_type=MESH)
 
-    @pl.loop(1, ny_dev)
-    def _(t):
+    for t in (1, ny_dev - 1):
         pl.semaphore_signal(barrier, inc=1, device_id={"gy": py(t)}, device_id_type=MESH)
-
-    for cp in small:
-        cp.wait()
-
-    r8 = rows_of((8, 128))
-    j8 = lax.rem(lanes((8, 128)), 8)
-    den = jnp.zeros((8, 128), f32)
-    thk = jnp.zeros((8, 128), f32)
-    for k in range(levels):
-        den = jnp.where(r8 == k, den_ref[k], den)
-        thk = jnp.where(r8 == k, thk_ref[k], thk)
-
-    def lift(a):
-        return jnp.where(r8 == 7, a, roll(a, -1, 0))
-
-    def below(a):
-        return jnp.where(r8 == 0, 0.0, roll(a, 1, 0))
-
-    lden = lift(den)
-    fd = (den + lden) / 2.0
-    fs = (thk + lift(thk)) / 2.0
-    mass = den * thk
-    zw = (DT / 60.0) / (fd * fs)
-    zt = (DT / 60.0) / mass
-    sc = (1.0 / DT) / mass
-    coefs = [lden * zw, below(lden) * zw, fd * zt, below(fd) * zt, fd * sc, below(fd) * sc, DT / fs]
-    for i, a in enumerate(coefs):
-        COEF[i * 8 : i * 8 + 8, :] = jnp.concatenate([a, a], axis=1)
-
-    cond = fd / fs
-    diag = jnp.sqrt(cond / mass)
-    off = -jnp.sqrt(cond / lift(mass))
-    b_mat = jnp.where(j8 == r8, diag, jnp.where(j8 == r8 + 1, off, 0.0))
-    q_mat = jnp.where(j8 == r8, 1.0, 0.0)
-    offsets = {}
-    for r in range(1, 8):
-        offsets[r] = sorted({((l ^ r) - l) % 8 for l in range(8)})
-
-    def partner(x, r):
-        out = None
-        lane = j8
-        for o in offsets[r]:
-            moved = roll(x, -o, 1)
-            sel = lax.rem(lane + o, 8) == (lane ^ r)
-            out = moved if out is None else jnp.where(sel, moved, out)
-        return out
-
-    def sweep(_, carry):
-        b, q = carry
-        for r in range(1, 8):
-            bp, qp = partner(b, r), partner(q, r)
-            al = jnp.sum(b * b, axis=0, keepdims=True)
-            ap = jnp.sum(bp * bp, axis=0, keepdims=True)
-            g = jnp.sum(b * bp, axis=0, keepdims=True)
-            d = ap - al
-            lane = j8[:1]
-            sg = jnp.where(d > 0.0, 2.0, jnp.where(d < 0.0, -2.0, jnp.where(lane < (lane ^ r), 2.0, -2.0)))
-            t = sg * g / (jnp.abs(d) + jnp.sqrt(d * d + 4.0 * g * g) + 1e-18)
-            c = 1.0 / jnp.sqrt(1.0 + t * t)
-            s = c * t
-            b, q = c * b - s * bp, c * q - s * qp
-        return b, q
-
-    b_mat, q_mat = lax.fori_loop(0, 5, sweep, (b_mat, q_mat))
-    lam = jnp.broadcast_to(jnp.sum(b_mat * b_mat, axis=0, keepdims=True), (8, 128))
-    root = jnp.sqrt(mass)
-    qf = q_mat * root
-    qi = q_mat / root
-    for j in range(8):
-        TF[j * 8 : j * 8 + 8, :] = jnp.broadcast_to(qf[:, j : j + 1], (8, 128))
-        TI[j * 8 : j * 8 + 8, :] = jnp.broadcast_to(qi[:, j : j + 1], (8, 128))
-        LAM[j] = jnp.broadcast_to(lam[:, j : j + 1], (8, 128))
+    for t in (1, n_chips - 1):
+        pl.semaphore_signal(barrier, inc=1, device_id={"gy": chip_at(t)}, device_id_type=MESH)
 
     for cp in loads[:4]:
         cp.wait()
@@ -272,7 +214,7 @@
         a, b = W[k, 8:16, :], TH[k, 8:16, :]
         YS_S[k] = jnp.where(row < 3, a, roll(b, 3, 0))
 
-    pl.semaphore_wait(barrier, nx_dev + ny_dev - 2)
+    pl.semaphore_wait(barrier, nx_dev - 1 + 4)
     halos = []
     for i, (src, dst, where) in enumerate(
         [
@@ -288,8 +230,97 @@
         )
         cp.start()
         halos.append(cp)
+
+    for cp in small:
+        cp.wait()
+
+    r8 = rows_of((8, 128))
+    j8 = lax.rem(lanes((8, 128)), 8)
+    den = jnp.zeros((8, 128), f32)
+    thk = jnp.zeros((8, 128), f32)
+    for k in range(levels):
+        den = jnp.where(r8 == k, den_ref[k], den)
+        thk = jnp.where(r8 == k, thk_ref[k], thk)
+
+    def lift(a):
+        return jnp.where(r8 == 7, a, roll(a, -1, 0))
+
+    def below(a):
+        return jnp.where(r8 == 0, 0.0, roll(a, 1, 0))
+
+    lden = lift(den)
+    fd = (den + lden) / 2.0
+    fs = (thk + lift(thk)) / 2.0
+    mass = den * thk
+    zw = (DT / 60.0) / (fd * fs)
+    zt = (DT / 60.0) / mass
+    sc = (1.0 / DT) / mass
+    coefs = [lden * zw, below(lden) * zw, fd * zt, below(fd) * zt, fd * sc, below(fd) * sc, DT / fs]
+    for i, a in enumerate(coefs):
+        COEF[i * 8 : i * 8 + 8, :] = jnp.concatenate([a, a], axis=1)
+
+    cond = fd / fs
+    diag = jnp.sqrt(cond / mass)
+    off = -jnp.sqrt(cond / lift(mass))
+    b_mat = jnp.where(j8 == r8, diag, jnp.where(j8 == r8 + 1, off, 0.0))
+    q_mat = jnp.where(j8 == r8, 1.0, 0.0)
+    pairs = [
+        (4, j8 < 4),
+        (1, lax.rem(j8, 2) == 0), (1, lax.rem(j8, 2) == 1),
+        (3, lax.rem(j8, 2) == 0), (3, lax.rem(j8, 2) == 1),
+        (2, lax.rem(j8, 4) < 2), (2, lax.rem(j8, 4) >= 2),
+    ]
+
+    def total(x):
+        return ((x[0] + x[1]) + (x[2] + x[3])) + ((x[4] + x[5]) + (x[6] + x[7]))
+
+    def partner(x, o, ahead):
+        if o == 4:
+            return roll(x, 4, 1)
+        return jnp.where(ahead, roll(x, -o, 1), roll(x, o, 1))
+
+    def sweep(_, carry):
+        b, q = list(carry[:8]), list(carry[8:])
+        for o, ahead in pairs:
+            bp = [partner(x, o, ahead) for x in b]
+            al = total([x * x for x in b])
+            ap = total([x * x for x in bp])
+            g = total([x * y for x, y in zip(b, bp)])
+            d = ap - al
+            h2 = d * d + 4.0 * g * g
+            ok = h2 > 1e-30
+            rh = lax.rsqrt(jnp.where(ok, h2, 1.0))
+            c2 = 0.5 + 0.5 * jnp.abs(d) * rh
+            rc = lax.rsqrt(c2)
+            sg = jnp.where(d > 0.0, g, jnp.where(d < 0.0, -g, jnp.where(ahead, g, -g)))
+            c = jnp.where(ok, c2 * rc, 1.0)
+            s = jnp.where(ok, sg * rh * rc, 0.0)
+            qp = [partner(x, o, ahead) for x in q]
+            b = [c * x - s * y for x, y in zip(b, bp)]
+            q = [c * x - s * y for x, y in zip(q, qp)]
+        return (*b, *q)
+
+    start = [jnp.broadcast_to(m[k : k + 1], (8, 128)) for m in (b_mat, q_mat) for k in range(8)]
+    got = lax.fori_loop(0, 5, sweep, tuple(start))
+    norm = 1.0 / total([x * x for x in got[8:]])
+    lam = total([x * x for x in got[:8]]) * norm
+    unit = jnp.sqrt(norm)
+    q_mat = jnp.zeros((8, 128), f32)
+    for k in range(8):
+        q_mat = jnp.where(r8 == k, got[8 + k] * unit, q_mat)
+    root = jnp.sqrt(mass)
+    qf = q_mat * root
+    qi = q_mat / root
+    for j in range(8):
+        TF[j * 8 : j * 8 + 8, :] = jnp.broadcast_to(qf[:, j : j + 1], (8, 128))
+        TI[j * 8 : j * 8 + 8, :] = jnp.broadcast_to(qi[:, j : j + 1], (8, 128))
+        LAM[j] = jnp.broadcast_to(lam[:, j : j + 1], (8, 128))
+
+    greet(0)
     for cp in halos:
         cp.wait()
+    greeted(0)
+    greet(1)
 
     for k in range(levels):
         n8, s8 = YN_R[k], YS_R[k]
@@ -421,6 +452,9 @@
             q, tend, fz = advect(TH, k, y0, 3, False, fz, 16)
             tn_ref[k, pl.ds(y0, YC), :] = q + tend
 
+    greeted(1)
+    greet(2)
+
     lam_g = LAM[gx]
     rate, scale = [], []
     for h in range(2):
@@ -456,10 +490,12 @@
                 S[h, pl.ds(y0 * 8 + m, YC, stride=8), :] = val[:, 128 * h : 128 * h + 128]
         a0, a1, b0, b1, p0, p1 = carry
         for i in range(YC):
-            f0 = S[0, pl.ds(y0 * 8 + 8 * i, 8), :]
-            f1 = S[1, pl.ds(y0 * 8 + 8 * i, 8), :]
+            at = pl.ds(y0 * 8 + 8 * i, 8)
+            f0, f1 = S[0, at, :], S[1, at, :]
             a0, a1 = f0 + rate[0] * a0, f1 + rate[1] * a1
             b0, b1 = b0 + p0 * f0, b1 + p1 * f1
+            SA[0, at, :], SA[1, at, :] = a0, a1
+            PWR[0, at, :], PWR[1, at, :] = p0, p1
             p0, p1 = p0 * rate[0], p1 * rate[1]
         return a0, a1, b0, b1, p0, p1
 
@@ -467,67 +503,74 @@
     one = jnp.ones((8, 128), f32)
     a0, a1, b0, b1, p0, p1 = lax.fori_loop(0, chunks, x_forward, (zero, zero, zero, zero, one, one))
 
-    half = 16
-    for h, (a, b, p) in enumerate([(a0, b0, p0), (a1, b1, p1)]):
-        for j in range(8):
-            IFS[h * 8 + j] = a[j : j + 1, :]
-            IFS[half + h * 8 + j] = b[j : j + 1, :]
-            RP[h * 8 + j] = p[j : j + 1, :]
-    IFR[0] = IFS[gy]
-
-    @pl.loop(1, ny_dev)
-    def _(t):
-        i = py(t)
-        slot = (ny_dev - t) + (i // half) * (2 * t - ny_dev)
-        send(IFS.at[i], IFR.at[slot], is_sem.at[0], ir_sem.at[0], {"gy": i}).start()
-
-    others = pl.ds(1, ny_dev - 1)
-    send(IFS.at[others], IFR.at[others], is_sem.at[0], ir_sem.at[0], {"gy": py(1)}).wait()
-    acc = IFR[...]
-    power = RP[lax.rem(gy, half)][None]
-    step = 1
-    while step < ny_dev:
-        acc = acc + power * jnp.concatenate([acc[ny_dev - step :], acc[: ny_dev - step]], axis=0)
-        power = power * power
-        step *= 2
-    acc = acc * (1.0 / (1.0 - power))
-    IFO[...] = jnp.concatenate([acc[ny_dev - 1 :], acc[: ny_dev - 1]], axis=0)
-    IFB[gy] = IFO[0]
-    sign = 1 - 2 * (gy // half)
-
-    @pl.loop(1, ny_dev)
-    def _(t):
-        dev = lax.rem(gy + t * sign + ny_dev, ny_dev)
-        send(IFO.at[t], IFB.at[gy], is_sem.at[1], ir_sem.at[1], {"gy": dev}).start()
-
-    send(IFO.at[others], IFB.at[others], is_sem.at[1], ir_sem.at[1], {"gy": py(1)}).wait()
-    ain = [jnp.concatenate([IFB[h * 8 + j] for j in range(8)], axis=0) for h in range(2)]
-    bin_ = [jnp.concatenate([IFB[half + h * 8 + j] for j in range(8)], axis=0) for h in range(2)]
+    greeted(2)
+
+    first = core == 0
+    whole = [p0, p1]
+    mine = []
+    for h, (a, b) in enumerate([(a0, b0), (a1, b1)]):
+        IFS[h] = jnp.where(first, a, b)
+        mine.append(jnp.where(first, b, a))
+    pair = {"gy": gy + 1 - 2 * core}
+    swap = send(IFS, IFR, is_sem.at[0], ir_sem.at[0], pair)
+    swap.start()
+    swap.wait()
+    for h in range(2):
+        CBS[h] = mine[h] + whole[h] * IFR[h]
+    sign = 2 * core - 1
+    for t in (4, 12, 11, 5, 3, 13, 10, 6, 2, 14, 8, 9, 7, 1, 15):
+        dev = 2 * lax.rem(chip + t * sign + n_chips, n_chips) + core
+        send(CBS, CBR.at[t], is_sem.at[1], ir_sem.at[1], {"gy": dev}).start()
 
     def back(i, carry):
         y = ny - 1 - i
         at = pl.ds(pl.multiple_of(y * 8, 8), 8)
         out = []
         for h in range(2):
-            b = S[h, at, :] + rate[h] * carry[h]
-            SB[h, at, :] = rate[h] * carry[h]
-            out.append(b)
+            b = rate[h] * carry[h]
+            SB[h, at, :] = SA[h, at, :] + b
+            out.append(S[h, at, :] + b)
         return tuple(out)
 
-    lax.fori_loop(0, ny, back, tuple(bin_), unroll=8)
-
-    def forth(y, carry):
-        at = pl.ds(pl.multiple_of(y * 8, 8), 8)
-        out = []
-        for h in range(2):
-            a = S[h, at, :] + rate[h] * carry[h]
-            S[h, at, :] = scale[h] * (a + SB[h, at, :])
-            out.append(a)
-        return tuple(out)
-
-    last = lax.fori_loop(0, ny, forth, tuple(ain), unroll=8)
+    lax.fori_loop(0, ny, back, (zero, zero), unroll=8)
+
+    others = pl.ds(1, n_chips - 1)
+    send(CBR.at[others], CBR.at[others], is_sem.at[1], ir_sem.at[1], pair).wait()
+    into = []
     for h in range(2):
-        S[h, ny * 8 : ny * 8 + 8, :] = scale[h] * (rate[h] * last[h] + bin_[h])
+        ratio = whole[h] * whole[h]
+        acc = CBS[h]
+        for t in range(n_chips - 1, 0, -1):
+            acc = CBR[t, h] + ratio * acc
+        full = ratio
+        n = 1
+        while n < n_chips:
+            full = full * full
+            n *= 2
+        into.append(acc / (1.0 - full))
+        INS[h] = into[h]
+    swap = send(INS, INR, is_sem.at[2], ir_sem.at[2], pair)
+    swap.start()
+    swap.wait()
+    ain, bin_ = [], []
+    for h in range(2):
+        own = IFR[h] + whole[h] * into[h]
+        ain.append(jnp.where(first, INR[h], own))
+        bin_.append(jnp.where(first, own, INR[h]))
+    ra = [rate[h] * ain[h] for h in range(2)]
+    rb = [rate[h] * bin_[h] for h in range(2)]
+
+    def correct(y0, n):
+        for i in range(n):
+            at = pl.ds(y0 * 8 + 8 * i, 8)
+            mirror = pl.ds((ny - 1 - i) * 8 - y0 * 8, 8)
+            for h in range(2):
+                S[h, at, :] = scale[h] * (SB[h, at, :] + PWR[h, at, :] * ra[h] + PWR[h, mirror, :] * rb[h])
+
+    end = slice((ny - 1) * 8, ny * 8)
+    for h in range(2):
+        last = SA[h, end, :] + PWR[h, end, :] * ra[h]
+        S[h, ny * 8 : ny * 8 + 8, :] = scale[h] * (rate[h] * last + bin_[h])
         S[h, ny * 8 + 8 : ny * 8 + 64, :] = jnp.zeros((56, 128), f32)
 
     def x_inverse(y0, n, put):
@@ -562,6 +605,7 @@
                 edge = jnp.where(lane_8 == d, roll(x[(2 * d + 2) % 16], d, 1), edge)
             EW[pl.ds(y0 + 8 * i, 8), :] = edge
 
+        correct(y0, YC)
         x_inverse(y0, YC, put)
         pltpu.make_async_copy(TX2.at[gx, c], RX2.at[c, gx], l2_sem.at[c]).start()
         for t in range(1, nx_dev):
@@ -591,37 +635,6 @@
         for t in range(1, nx_dev):
             g = px(t)
             send(TX2.at[g, c], RX2.at[c, g], s2_sem.at[c, t], r2_sem.at[c, g], {"gx": g}).wait_recv()
-
-    pltpu.make_async_copy(X2.at[gx], XR.at[gx], l2_sem.at[chunks]).wait()
-    for t in range(1, nx_dev):
-        g = px(t)
-        send(X2.at[g], XR.at[g], sx_sem.at[t], rx_sem.at[g], {"gx": g}).wait_recv()
-
-    @pl.loop(0, chunks)
-    def _(c):
-        for t in range(1, nx_dev):
-            g = px(t)
-            send(TX1.at[g, c], RX1.at[c, g], s1_sem.at[c, t], r1_sem.at[c, g], {"gx": g}).wait_send()
-            send(TX2.at[g, c], RX2.at[c, g], s2_sem.at[c, t], r2_sem.at[c, g], {"gx": g}).wait_send()
-
-    for t in range(1, nx_dev):
-        g = px(t)
-        send(X2.at[g], XR.at[g], sx_sem.at[t], rx_sem.at[g], {"gx": g}).wait_send()
-
-
-def finish(
-    U, V, WS, tn_ref, RX2, XR, TI, COEF, un_hbm, vn_hbm, wn_hbm, tn_hbm, p_hbm,
-    un_ref, vn_ref, wn_ref, p_ref, EC, EX, tn_sem, out_sem,
-):
-    levels, ny, nx = U.shape
-    chunks = ny // YC
-    theta = pltpu.make_async_copy(tn_ref, tn_hbm, tn_sem.at[0])
-    theta.start()
-    lane_n = lanes((ny, 128))
-    row8 = rows_of((8, 128))
-
-    @pl.loop(0, chunks)
-    def _(c):
         cen = pl.ds(pl.multiple_of(c * YC, YC), YC)
         for h in range(2):
             col = [RX2[c, j, h] for j in range(levels)]
@@ -630,6 +643,33 @@
                 for j in range(1, levels):
                     acc = acc + TI[j * 8 + k : j * 8 + k + 1, :] * col[j]
                 p_ref[k, cen, 128 * h : 128 * h + 128] = acc
+
+    pltpu.make_async_copy(X2.at[gx], XR.at[gx], l2_sem.at[chunks]).wait()
+    for t in range(1, nx_dev):
+        g = px(t)
+        send(X2.at[g], XR.at[g], sx_sem.at[t], rx_sem.at[g], {"gx": g}).wait_recv()
+
+    @pl.loop(0, chunks)
+    def _(c):
+        for t in range(1, nx_dev):
+            g = px(t)
+            send(TX1.at[g, c], RX1.at[c, g], s1_sem.at[c, t], r1_sem.at[c, g], {"gx": g}).wait_send()
+            send(TX2.at[g, c], RX2.at[c, g], s2_sem.at[c, t], r2_sem.at[c, g], {"gx": g}).wait_send()
+
+    for t in range(1, nx_dev):
+        g = px(t)
+        send(X2.at[g], XR.at[g], sx_sem.at[t], rx_sem.at[g], {"gx": g}).wait_send()
+
+
+def finish(
+    U, V, WS, tn_ref, p_ref, XR, TI, COEF, un_hbm, vn_hbm, wn_hbm, tn_hbm, p_hbm,
+    un_ref, vn_ref, wn_ref, EC, EX, tn_sem, out_sem,
+):
+    levels, ny, nx = U.shape
+    theta = pltpu.make_async_copy(tn_ref, tn_hbm, tn_sem.at[0])
+    theta.start()
+    lane_n = lanes((ny, 128))
+    row8 = rows_of((8, 128))
 
     def out(i, ref, hbm, k):
         return pltpu.make_async_copy(ref.at[k], hbm.at[k], out_sem.at[i, k])
@@ -707,16 +747,20 @@
         vm((8 * YC, 256), f32),
         vm((2, (ny + 8) * 8, 128), f32),
         vm((2, ny * 8, 128), f32),
-        vm((32, 1, 128), f32), vm((32, 1, 128), f32), vm((32, 1, 128), f32), vm((32, 1, 128), f32),
-        vm((16, 1, 128), f32),
+        vm((2, ny * 8, 128), f32),
+        vm((2, ny * 8, 128), f32),
+        vm((2, 8, 128), f32), vm((2, 8, 128), f32), vm((2, 8, 128), f32),
+        vm((ny_dev // 2, 2, 8, 128), f32),
+        vm((2, 8, 128), f32), vm((2, 8, 128), f32),
         vm((nx_dev, chunks, 2, YC, 128), f32),
+        vm((chunks, levels, 2, YC, 128), f32),
         vm((nx_dev, 8, 128), f32),
         vm((128, 128), f32),
         dma((8,)), dma((4,)), dma((4,)),
         dma((chunks, nx_dev)), dma((chunks, nx_dev)), dma((chunks,)),
-        dma((2,)), dma((2,)),
+        dma((3,)), dma((3,)),
         dma((chunks, nx_dev)), dma((chunks, nx_dev)), dma((chunks + 1,)),
-        dma((nx_dev,)), dma((nx_dev,)),
+        dma((nx_dev,)), dma((nx_dev,)), pltpu.SemaphoreType.REGULAR((3,)),
     ]
     mid = pl.pallas_call(
         functools.partial(kernel, nx_dev, ny_dev),
@@ -725,7 +769,7 @@
             jax.ShapeDtypeStruct((levels, ny + 8, nx), f32),
             out,
             out,
-            jax.ShapeDtypeStruct((chunks, levels, 2, YC, 128), f32),
+            out,
             jax.ShapeDtypeStruct((levels, 8, 128), f32),
             jax.ShapeDtypeStruct((64, 128), f32),
             jax.ShapeDtypeStruct((56, 256), f32),
@@ -747,7 +791,7 @@
         in_specs=[vmem] * 8,
         out_specs=(hbm,) * 5,
         scratch_shapes=[
-            vm(full, f32), vm(full, f32), vm(full, f32), vm(full, f32),
+            vm(full, f32), vm(full, f32), vm(full, f32),
             vm((128, 128), f32), vm((levels, 8, 128), f32), dma((1,)), dma((4, levels)),
         ],
         compiler_params=pltpu.CompilerParams(vmem_limit_bytes=24 << 20),

time: 51.1 us -> 49.2 us (0.963)
  Pallas kernels: 50.3 us -> 48.4 us
    pallas_call x1, Pallas kernels: 48.4 us -> 46.6 us  [per_device(): pl.pallas_call(functools.partial(kernel, nx_dev, ny_dev), out_shape=(out,...]
where the time goes in v2:
time: 49.2 us; the launch traced here: 49.1 us
  Pallas kernels  48.4 us (98%)
  between operations  0.64 us (1%)
    pallas_call x1, Pallas kernels, per_device(): pl.pallas_call(functools.partial(kernel, nx_dev, ny_dev), out_shape=(out,...  46.6 us
    pallas_call x1, Pallas kernels, per_device(): pl.pallas_call(finish, out_shape=(out,) * 5, in_specs=[vmem] * 8, out_spe...  1.8 us

profile of v2, /device:TPU:1, one launch (start us, length us, event | category | flops | bytes accessed | tf_op | source)
XLA Modules:
  0.0 49.1 jit_solution(18153108993497208218)
XLA Ops:
  0.6 46.6 %substep.1 = (f32[8,64,256]{2,1,0:T(8,128)S(1)}, f32[8,72,256]{2,1,0:T(8,128)S(1)}, f32[8,64,256]{2,1,0:T(8,128)S(1)}, f32[8,64,256]{2,1,0:T(8,128)S(1)}, f32[8,...) custom-call(f32[8]{0:T(128)} %den_hbm.1, f32[8]{0:T(128)} %thk_hbm.1, ...), custom_call_target="tpu_custom_call" | custom-call | tf_op jit(solution)/shard_map/substep/pallas_call | solution.py:765
  47.3 1.8 %finish.1 = (f32[8,64,256]{2,1,0:T(8,128)}, f32[8,64,256]{2,1,0:T(8,128)}, f32[8,64,256]{2,1,0:T(8,128)}, f32[8,64,256]{2,1,0:T(8,128)}, f32[8,64,256]{2,1,0:T(8,128)}) custom-call(f32[8,64,256]{2,1,0:T(8,128)S(1)} %get-tuple-element.13.U, f32[8,72,256]{2,1,0:T(8,128)S(1)} %get-tuple-element.14.V, f32[8,64,256]{2,1,0:T(8,128)S(1)} %get-tuple-element.15.WS, ...), custom_call_target="tpu_custom_call" | custom-call | tf_op jit(solution)/shard_map/finish/pallas_call | solution.py:788

commit v3 on v2

--- a/solution.py
+++ b/solution.py
@@ -128,12 +128,12 @@
 def kernel(
     nx_dev, ny_dev,
     den_hbm, thk_hbm, tab_hbm, u_hbm, v_hbm, w_hbm, th_hbm, mats_hbm,
-    U, V, WS, tn_ref, p_ref, XR, TI, COEF,
-    den_ref, thk_ref, tab_ref, W, TH, MATS, TF, LAM,
+    U, V, WS, tn_ref, p_ref, XR, TI,
+    den_ref, thk_ref, tab_ref, COEF, W, TH, MATS, TF, LAM,
     PE_S, PW_S, PE_R, PW_R, YN_S, YS_S, YN_R, YS_R, FPK, FYP,
     SRC, TX1, RX1, Z, S, SA, SB, PWR, IFS, IFR, CBS, CBR, INS, INR, TX2, RX2, X2, EW,
     in_sem, hs_sem, hr_sem, s1_sem, r1_sem, l1_sem, is_sem, ir_sem, s2_sem, r2_sem, l2_sem,
-    sx_sem, rx_sem, near_sem,
+    sx_sem, rx_sem,
 ):
     gx = lax.axis_index("gx")
     gy = lax.axis_index("gy")
@@ -151,13 +151,6 @@
 
     def chip_at(t):
         return 2 * lax.rem(chip + t, n_chips) + core
-
-    def greet(stage):
-        for t in (2**stage, n_chips - 2**stage):
-            pl.semaphore_signal(near_sem.at[stage], inc=1, device_id={"gy": chip_at(t)}, device_id_type=MESH)
-
-    def greeted(stage):
-        pl.semaphore_wait(near_sem.at[stage], 2)
 
     mid = pl.ds(8, ny)
     small = [
@@ -181,55 +174,8 @@
 
     for t in (1, ny_dev - 1):
         pl.semaphore_signal(barrier, inc=1, device_id={"gy": py(t)}, device_id_type=MESH)
-    for t in (1, n_chips - 1):
+    for t in range(1, n_chips):
         pl.semaphore_signal(barrier, inc=1, device_id={"gy": chip_at(t)}, device_id_type=MESH)
-
-    for cp in loads[:4]:
-        cp.wait()
-    lane_c = lanes((YC, 128))
-
-    @pl.loop(0, chunks)
-    def _(c):
-        y0 = pl.multiple_of(c * YC, YC)
-        east = jnp.zeros((YC, 128), f32)
-        west = jnp.zeros((YC, 128), f32)
-        for k in range(levels):
-            o = 16 * k
-            rows = pl.ds(y0 + 8, YC)
-            wl, wr = W[k, rows, 0:128], W[k, rows, 128:256]
-            tl, tr = TH[k, rows, 0:128], TH[k, rows, 128:256]
-            ur = U[k, pl.ds(y0, YC), 128:256]
-            east = jnp.where((lane_c >= o) & (lane_c < o + 3), roll(wr, o - 125, 1), east)
-            east = jnp.where((lane_c >= o + 3) & (lane_c < o + 6), roll(tr, o + 3 - 125, 1), east)
-            east = jnp.where(lane_c == o + 6, roll(ur, o + 6 - 127, 1), east)
-            west = jnp.where((lane_c >= o) & (lane_c < o + 3), roll(wl, o, 1), west)
-            west = jnp.where((lane_c >= o + 3) & (lane_c < o + 6), roll(tl, o + 3, 1), west)
-        PE_S[pl.ds(y0, YC), :] = east
-        PW_S[pl.ds(y0, YC), :] = west
-
-    for k in range(levels):
-        a, b, c = W[k, ny : ny + 8, :], TH[k, ny : ny + 8, :], V[k, ny : ny + 8, :]
-        row = rows_of((8, nx))
-        YN_S[k] = jnp.where(row < 3, roll(a, 3, 0), jnp.where(row < 6, roll(b, 6, 0), roll(c, 7, 0)))
-        a, b = W[k, 8:16, :], TH[k, 8:16, :]
-        YS_S[k] = jnp.where(row < 3, a, roll(b, 3, 0))
-
-    pl.semaphore_wait(barrier, nx_dev - 1 + 4)
-    halos = []
-    for i, (src, dst, where) in enumerate(
-        [
-            (PE_S, PE_R, {"gx": px(1)}),
-            (PW_S, PW_R, {"gx": px(nx_dev - 1)}),
-            (YN_S, YN_R, {"gy": py(1)}),
-            (YS_S, YS_R, {"gy": py(ny_dev - 1)}),
-        ]
-    ):
-        cp = pltpu.make_async_remote_copy(
-            src_ref=src, dst_ref=dst, send_sem=hs_sem.at[i], recv_sem=hr_sem.at[i],
-            device_id=where, device_id_type=MESH,
-        )
-        cp.start()
-        halos.append(cp)
 
     for cp in small:
         cp.wait()
@@ -316,11 +262,76 @@
         TI[j * 8 : j * 8 + 8, :] = jnp.broadcast_to(qi[:, j : j + 1], (8, 128))
         LAM[j] = jnp.broadcast_to(lam[:, j : j + 1], (8, 128))
 
-    greet(0)
+    for cp in loads[:4]:
+        cp.wait()
+    lane_c = lanes((YC, 128))
+
+    @pl.loop(0, chunks)
+    def _(c):
+        y0 = pl.multiple_of(c * YC, YC)
+        east = jnp.zeros((YC, 128), f32)
+        west = jnp.zeros((YC, 128), f32)
+        for k in range(levels):
+            o = 16 * k
+            rows = pl.ds(y0 + 8, YC)
+            wl, wr = W[k, rows, 0:128], W[k, rows, 128:256]
+            tl, tr = TH[k, rows, 0:128], TH[k, rows, 128:256]
+            ur = U[k, pl.ds(y0, YC), 128:256]
+            east = jnp.where((lane_c >= o) & (lane_c < o + 3), roll(wr, o - 125, 1), east)
+            east = jnp.where((lane_c >= o + 3) & (lane_c < o + 6), roll(tr, o + 3 - 125, 1), east)
+            east = jnp.where(lane_c == o + 6, roll(ur, o + 6 - 127, 1), east)
+            west = jnp.where((lane_c >= o) & (lane_c < o + 3), roll(wl, o, 1), west)
+            west = jnp.where((lane_c >= o + 3) & (lane_c < o + 6), roll(tl, o + 3, 1), west)
+        PE_S[pl.ds(y0, YC), :] = east
+        PW_S[pl.ds(y0, YC), :] = west
+
+    for k in range(levels):
+        a, b, c = W[k, ny : ny + 8, :], TH[k, ny : ny + 8, :], V[k, ny : ny + 8, :]
+        row = rows_of((8, nx))
+        YN_S[k] = jnp.where(row < 3, roll(a, 3, 0), jnp.where(row < 6, roll(b, 6, 0), roll(c, 7, 0)))
+        a, b = W[k, 8:16, :], TH[k, 8:16, :]
+        YS_S[k] = jnp.where(row < 3, a, roll(b, 3, 0))
+
+    pl.semaphore_wait(barrier, nx_dev - 1 + 2 + n_chips - 1)
+    halos = []
+    for i, (src, dst, where) in enumerate(
+        [
+            (PE_S, PE_R, {"gx": px(1)}),
+            (PW_S, PW_R, {"gx": px(nx_dev - 1)}),
+            (YN_S, YN_R, {"gy": py(1)}),
+            (YS_S, YS_R, {"gy": py(ny_dev - 1)}),
+        ]
+    ):
+        cp = pltpu.make_async_remote_copy(
+            src_ref=src, dst_ref=dst, send_sem=hs_sem.at[i], recv_sem=hr_sem.at[i],
+            device_id=where, device_id_type=MESH,
+        )
+        cp.start()
+        halos.append(cp)
+
+    def nxt(k):
+        return min(k + 1, levels - 1)
+
+    def z_part(field, k, rows, w, fz_below, zi):
+        zq = [field[min(max(k + s, 0), levels - 1), rows, :] for s in range(-2, 4)]
+        fz = flux(*zq, w)
+        tend = COEF[zi + k : zi + k + 1, :] * fz
+        if k > 0:
+            tend = tend - COEF[zi + 8 + k : zi + 9 + k, :] * fz_below
+        return tend, fz
+
+    @pl.loop(0, chunks)
+    def _(c):
+        y0 = pl.multiple_of(c * YC, YC)
+        rows = pl.ds(y0 + 8, YC)
+        fz = None
+        for k in range(levels):
+            w, w1 = W[k, rows, :], W[nxt(k), rows, :]
+            tend, fz = z_part(W, k, rows, (w + w1) / 2.0, fz, 0)
+            WS[k, pl.ds(y0, YC), :] = w - tend + (0.5 * DT) * (TH[k, rows, :] + TH[nxt(k), rows, :])
+
     for cp in halos:
         cp.wait()
-    greeted(0)
-    greet(1)
 
     for k in range(levels):
         n8, s8 = YN_R[k], YS_R[k]
@@ -341,9 +352,6 @@
         jnp.where(lane_m == 0, u_w, u_th),
     )
 
-    def nxt(k):
-        return min(k + 1, levels - 1)
-
     def y_shifts(block, n):
         return [roll(block, -s, 0)[8 : 8 + n] if s else block[8 : 8 + n] for s in range(-2, 4)]
 
@@ -356,7 +364,7 @@
                 c = (c + V[nxt(k), 0:8, :]) / 2.0
             FYP[k] = flux(*qs, c)
 
-    def advect(field, k, y0, extra, lifted, fz_below, zi):
+    def horizontal(field, k, y0, extra, lifted):
         o = 16 * k + extra
         rows = pl.ds(y0 + 8, YC)
         cen = pl.ds(y0, YC)
@@ -377,11 +385,10 @@
             else:
                 ls.append(jnp.where(lane_c >= -s, a, roll(pw, -s - 3 - o, 1)))
                 rs.append(jnp.where(lane_c >= -s, b, a))
-        u, v, w = U[k, cen, :], V[k, rows, :], W[k, rows, :]
+        u, v = U[k, cen, :], V[k, rows, :]
         if lifted:
             u = (u + U[nxt(k), cen, :]) / 2.0
             v = (v + V[nxt(k), rows, :]) / 2.0
-            w = (w + W[nxt(k), rows, :]) / 2.0
         fl = flux(*ls, u[:, :128])
         fr = flux(*rs, u[:, 128:])
         fl_roll = roll(fl, 1, 1)
@@ -392,12 +399,7 @@
         prev = roll(jnp.concatenate([FYP[k], fy], axis=0), 1, 0)[8:]
         FYP[k] = fy[YC - 8 :]
         div = div + (fy - prev)
-        zq = [field[min(max(k + s, 0), levels - 1), rows, :] for s in range(-2, 4)]
-        fz = flux(*zq, w)
-        tend = (-DT / 60.0) * div - COEF[zi + k : zi + k + 1, :] * fz
-        if k > 0:
-            tend = tend + COEF[zi + 8 + k : zi + 9 + k, :] * fz_below
-        return q, tend, fz
+        return (-DT / 60.0) * div
 
     def send(src, dst, s_sem, r_sem, who):
         return pltpu.make_async_remote_copy(
@@ -410,12 +412,10 @@
     @pl.loop(0, chunks)
     def _(c):
         y0 = pl.multiple_of(c * YC, YC)
-        rows = pl.ds(y0 + 8, YC)
         cen = pl.ds(y0, YC)
-        fz, star_below = None, None
+        star_below = None
         for k in range(levels):
-            q, tend, fz = advect(W, k, y0, 0, True, fz, 0)
-            star = q + tend + (0.5 * DT) * (TH[k, rows, :] + TH[nxt(k), rows, :])
+            star = WS[k, cen, :] + horizontal(W, k, y0, 0, True)
             WS[k, cen, :] = star
             u = U[k, cen, :]
             ul = roll(u[:, :128], 1, 1)
@@ -449,11 +449,9 @@
         y0 = pl.multiple_of(c * YC, YC)
         fz = None
         for k in range(levels):
-            q, tend, fz = advect(TH, k, y0, 3, False, fz, 16)
-            tn_ref[k, pl.ds(y0, YC), :] = q + tend
-
-    greeted(1)
-    greet(2)
+            rows = pl.ds(y0 + 8, YC)
+            tend, fz = z_part(TH, k, rows, W[k, rows, :], fz, 16)
+            tn_ref[k, pl.ds(y0, YC), :] = TH[k, rows, :] - tend + horizontal(TH, k, y0, 3, False)
 
     lam_g = LAM[gx]
     rate, scale = [], []
@@ -503,8 +501,6 @@
     one = jnp.ones((8, 128), f32)
     a0, a1, b0, b1, p0, p1 = lax.fori_loop(0, chunks, x_forward, (zero, zero, zero, zero, one, one))
 
-    greeted(2)
-
     first = core == 0
     whole = [p0, p1]
     mine = []
@@ -643,6 +639,10 @@
                 for j in range(1, levels):
                     acc = acc + TI[j * 8 + k : j * 8 + k + 1, :] * col[j]
                 p_ref[k, cen, 128 * h : 128 * h + 128] = acc
+        for k in range(levels):
+            g = COEF[48 + k : 49 + k, :]
+            step = p_ref[k + 1, cen, :] - p_ref[k, cen, :] if k + 1 < levels else -p_ref[k, cen, :]
+            WS[k, cen, :] = WS[k, cen, :] - g * step
 
     pltpu.make_async_copy(X2.at[gx], XR.at[gx], l2_sem.at[chunks]).wait()
     for t in range(1, nx_dev):
@@ -662,8 +662,8 @@
 
 
 def finish(
-    U, V, WS, tn_ref, p_ref, XR, TI, COEF, un_hbm, vn_hbm, wn_hbm, tn_hbm, p_hbm,
-    un_ref, vn_ref, wn_ref, EC, EX, tn_sem, out_sem,
+    U, V, WS, tn_ref, p_ref, XR, TI, un_hbm, vn_hbm, wn_hbm, tn_hbm, p_hbm,
+    un_ref, vn_ref, EC, EX, tn_sem, out_sem,
 ):
     levels, ny, nx = U.shape
     theta = pltpu.make_async_copy(tn_ref, tn_hbm, tn_sem.at[0])
@@ -674,9 +674,10 @@
     def out(i, ref, hbm, k):
         return pltpu.make_async_copy(ref.at[k], hbm.at[k], out_sem.at[i, k])
 
-    outs = [(p_ref, p_hbm), (un_ref, un_hbm), (vn_ref, vn_hbm), (wn_ref, wn_hbm)]
+    outs = [(p_ref, p_hbm), (un_ref, un_hbm), (vn_ref, vn_hbm), (WS, wn_hbm)]
     for k in range(levels):
         out(0, p_ref, p_hbm, k).start()
+        out(3, WS, wn_hbm, k).start()
 
     east = jnp.zeros((8, 128), f32)
     for k in range(levels):
@@ -704,12 +705,6 @@
         shifted = jnp.where(rows_of((ny, nx)) < ny - 1, shifted, jnp.broadcast_to(north, (ny, nx)))
         vn_ref[k] = V[k, 8 : 8 + ny, :] - DT * (shifted - p)
         out(2, vn_ref, vn_hbm, k).start()
-        g = COEF[48 + k : 49 + k, :]
-        if k + 1 < levels:
-            wn_ref[k] = WS[k] - g * (p_ref[k + 1] - p)
-        else:
-            wn_ref[k] = WS[k] + g * p
-        out(3, wn_ref, wn_hbm, k).start()
 
     theta.wait()
     for k in range(levels):
@@ -731,6 +726,7 @@
     vmem = pl.BlockSpec(memory_space=pltpu.VMEM)
     scratch = [
         pltpu.SMEM((levels,), f32), pltpu.SMEM((levels,), f32), vm((32, 128), f32),
+        vm((56, 256), f32),
         vm((levels, ny + 16, nx), f32),
         vm((levels, ny + 16, nx), f32),
         vm((8, 256, 256), bf16),
@@ -760,7 +756,7 @@
         dma((chunks, nx_dev)), dma((chunks, nx_dev)), dma((chunks,)),
         dma((3,)), dma((3,)),
         dma((chunks, nx_dev)), dma((chunks, nx_dev)), dma((chunks + 1,)),
-        dma((nx_dev,)), dma((nx_dev,)), pltpu.SemaphoreType.REGULAR((3,)),
+        dma((nx_dev,)), dma((nx_dev,)),
     ]
     mid = pl.pallas_call(
         functools.partial(kernel, nx_dev, ny_dev),
@@ -772,10 +768,9 @@
             out,
             jax.ShapeDtypeStruct((levels, 8, 128), f32),
             jax.ShapeDtypeStruct((64, 128), f32),
-            jax.ShapeDtypeStruct((56, 256), f32),
         ),
         in_specs=[hbm] * 8,
-        out_specs=(vmem,) * 8,
+        out_specs=(vmem,) * 7,
         scratch_shapes=scratch,
         compiler_params=pltpu.CompilerParams(
             collective_id=0, has_side_effects=True, vmem_limit_bytes=36 << 20
@@ -788,10 +783,10 @@
     return pl.pallas_call(
         finish,
         out_shape=(out,) * 5,
-        in_specs=[vmem] * 8,
+        in_specs=[vmem] * 7,
         out_specs=(hbm,) * 5,
         scratch_shapes=[
-            vm(full, f32), vm(full, f32), vm(full, f32),
+            vm(full, f32), vm(full, f32),
             vm((128, 128), f32), vm((levels, 8, 128), f32), dma((1,)), dma((4, levels)),
         ],
         compiler_params=pltpu.CompilerParams(vmem_limit_bytes=24 << 20),

time: 49.2 us -> 48.6 us (0.988)
  Pallas kernels: 48.4 us -> 47.8 us
    pallas_call x1, Pallas kernels: 46.6 us -> 46.1 us  [per_device(): pl.pallas_call(functools.partial(kernel, nx_dev, ny_dev), out_shape=(out,...]
where the time goes in v3:
time: 48.6 us; the launch traced here: 48.5 us
  Pallas kernels  47.8 us (98%)
  between operations  0.64 us (1%)
    pallas_call x1, Pallas kernels, per_device(): pl.pallas_call(functools.partial(kernel, nx_dev, ny_dev), out_shape=(out,...  46.1 us
    pallas_call x1, Pallas kernels, per_device(): pl.pallas_call(finish, out_shape=(out,) * 5, in_specs=[vmem] * 7, out_spe...  1.75 us

profile of v3, /device:TPU:1, one launch (start us, length us, event | category | flops | bytes accessed | tf_op | source)
XLA Modules:
  0.0 48.5 jit_solution(13849820771097710409)
XLA Ops:
  0.6 46.1 %substep.1 = (f32[8,64,256]{2,1,0:T(8,128)S(1)}, f32[8,72,256]{2,1,0:T(8,128)S(1)}, f32[8,64,256]{2,1,0:T(8,128)S(1)}, f32[8,64,256]{2,1,0:T(8,128)S(1)}, f32[8,...) custom-call(f32[8]{0:T(128)} %den_hbm.1, f32[8]{0:T(128)} %thk_hbm.1, ...), custom_call_target="tpu_custom_call" | custom-call | tf_op jit(solution)/shard_map/substep/pallas_call | solution.py:761
  46.7 1.8 %finish.1 = (f32[8,64,256]{2,1,0:T(8,128)}, f32[8,64,256]{2,1,0:T(8,128)}, f32[8,64,256]{2,1,0:T(8,128)}, f32[8,64,256]{2,1,0:T(8,128)}, f32[8,64,256]{2,1,0:T(8,128)}) custom-call(f32[8,64,256]{2,1,0:T(8,128)S(1)} %get-tuple-element.12.U, f32[8,72,256]{2,1,0:T(8,128)S(1)} %get-tuple-element.13.V, f32[8,64,256]{2,1,0:T(8,128)S(1)} %get-tuple-element.14.WS, ...), custom_call_target="tpu_custom_call" | custom-call | tf_op jit(solution)/shard_map/finish/pallas_call | solution.py:783

commit v4 on v3

--- a/solution.py
+++ b/solution.py
@@ -247,20 +247,7 @@
         return (*b, *q)
 
     start = [jnp.broadcast_to(m[k : k + 1], (8, 128)) for m in (b_mat, q_mat) for k in range(8)]
-    got = lax.fori_loop(0, 5, sweep, tuple(start))
-    norm = 1.0 / total([x * x for x in got[8:]])
-    lam = total([x * x for x in got[:8]]) * norm
-    unit = jnp.sqrt(norm)
-    q_mat = jnp.zeros((8, 128), f32)
-    for k in range(8):
-        q_mat = jnp.where(r8 == k, got[8 + k] * unit, q_mat)
-    root = jnp.sqrt(mass)
-    qf = q_mat * root
-    qi = q_mat / root
-    for j in range(8):
-        TF[j * 8 : j * 8 + 8, :] = jnp.broadcast_to(qf[:, j : j + 1], (8, 128))
-        TI[j * 8 : j * 8 + 8, :] = jnp.broadcast_to(qi[:, j : j + 1], (8, 128))
-        LAM[j] = jnp.broadcast_to(lam[:, j : j + 1], (8, 128))
+    got = lax.fori_loop(0, 1, sweep, tuple(start))
 
     for cp in loads[:4]:
         cp.wait()
@@ -308,6 +295,21 @@
         )
         cp.start()
         halos.append(cp)
+
+    got = lax.fori_loop(0, 4, sweep, got)
+    norm = 1.0 / total([x * x for x in got[8:]])
+    lam = total([x * x for x in got[:8]]) * norm
+    unit = jnp.sqrt(norm)
+    q_mat = jnp.zeros((8, 128), f32)
+    for k in range(8):
+        q_mat = jnp.where(r8 == k, got[8 + k] * unit, q_mat)
+    root = jnp.sqrt(mass)
+    qf = q_mat * root
+    qi = q_mat / root
+    for j in range(8):
+        TF[j * 8 : j * 8 + 8, :] = jnp.broadcast_to(qf[:, j : j + 1], (8, 128))
+        TI[j * 8 : j * 8 + 8, :] = jnp.broadcast_to(qi[:, j : j + 1], (8, 128))
+        LAM[j] = jnp.broadcast_to(lam[:, j : j + 1], (8, 128))
 
     def nxt(k):
         return min(k + 1, levels - 1)

time: 48.6 us -> 46.2 us (0.951)
  Pallas kernels: 47.8 us -> 45.5 us
    pallas_call x1, Pallas kernels: 46.1 us -> 43.8 us  [per_device(): pl.pallas_call(functools.partial(kernel, nx_dev, ny_dev), out_shape=(out,...]
where the time goes in v4:
time: 46.2 us; the launch traced here: 46.1 us
  Pallas kernels  45.5 us (98%)
  between operations  0.64 us (1%)
    pallas_call x1, Pallas kernels, per_device(): pl.pallas_call(functools.partial(kernel, nx_dev, ny_dev), out_shape=(out,...  43.8 us
    pallas_call x1, Pallas kernels, per_device(): pl.pallas_call(finish, out_shape=(out,) * 5, in_specs=[vmem] * 7, out_spe...  1.75 us

profile of v4, /device:TPU:1, one launch (start us, length us, event | category | flops | bytes accessed | tf_op | source)
XLA Modules:
  0.0 46.1 jit_solution(3521604279723922536)
XLA Ops:
  0.6 43.8 %substep.1 = (f32[8,64,256]{2,1,0:T(8,128)S(1)}, f32[8,72,256]{2,1,0:T(8,128)S(1)}, f32[8,64,256]{2,1,0:T(8,128)S(1)}, f32[8,64,256]{2,1,0:T(8,128)S(1)}, f32[8,...) custom-call(f32[8]{0:T(128)} %den_hbm.1, f32[8]{0:T(128)} %thk_hbm.1, ...), custom_call_target="tpu_custom_call" | custom-call | tf_op jit(solution)/shard_map/substep/pallas_call | solution.py:763
  44.4 1.8 %finish.1 = (f32[8,64,256]{2,1,0:T(8,128)}, f32[8,64,256]{2,1,0:T(8,128)}, f32[8,64,256]{2,1,0:T(8,128)}, f32[8,64,256]{2,1,0:T(8,128)}, f32[8,64,256]{2,1,0:T(8,128)}) custom-call(f32[8,64,256]{2,1,0:T(8,128)S(1)} %get-tuple-element.12.U, f32[8,72,256]{2,1,0:T(8,128)S(1)} %get-tuple-element.13.V, f32[8,64,256]{2,1,0:T(8,128)S(1)} %get-tuple-element.14.WS, ...), custom_call_target="tpu_custom_call" | custom-call | tf_op jit(solution)/shard_map/finish/pallas_call | solution.py:785
